TPU v7x, 512 devices: a whole 4x4x16 slice. The times are simulated.
512 devices in a mesh: row: 32 (over z, core), col: 4 (over y), mem: 4 (over x).
Axes of the slice: x: 4, y: 4, z: 16, core: 2. Of those that a mesh axis runs over, the one named last changes fastest.
Arguments:
- adj_final: float32 [16384, 4096], P(('mem', 'row'), 'col'), parts along dimension 0, may hold values from -6 to 6
- kappa: float32 [16384, 4096], P(('mem', 'row'), 'col'), parts along dimension 0, may hold values from 0.1 to 1
- elev_early: float32 [16384, 4096], P(('mem', 'row'), 'col'), parts along dimension 0, may hold values from -6 to 6
- elev_late: float32 [16384, 4096], P(('mem', 'row'), 'col'), parts along dimension 0, may hold values from -6 to 6
- basis: bfloat16 [128, 4, 4, 1024, 256], P(('mem', 'row'), 'col'), parts along dimension 0, may hold values from -0.1875 to 0.1875
- basis_index: int32 [128, 4, 512], P(('mem', 'row'), 'col'), parts along dimension 0, may hold values from 0 to 3
- intersection_patch: int32 [128, 4, 512], P(('mem', 'row'), 'col'), parts along dimension 0, may hold values from 0 to 2047, as said below
- owner_row: int32 [16, 2048], P(('mem', 'col')), parts along dimension 0, may hold values from 0 to 2047, as said below
Outputs:
- adj_start: float32 [16384, 4096], P(('mem', 'row'), 'col'), parts along dimension 0
- coeff_grad: float32 [16, 2048, 256], P(('mem', 'col'), 'row'), parts along dimension 0
There are 4 independent parts, one for each index of `mem`. A program takes and returns all parts, laid end to end along the dimension named above; each array names one. Nothing has to cross between parts.
Inputs may be any that keep to these rules, and one draw needn't show every extreme that they name: Each row of owner_row is a permutation of 0 to 2047; the owner of patch p in strip j is owner_row[j, p] // 64. `intersection_patch`: of the 512 entries of one tile (i, j), at most 32 name patches of any one owner r (patches p with owner_row[j, p] // 64 = r), and exactly 32 name patches of some owner.
All inputs are finite; a program needn't handle non-finite values.
Results may differ from a plain program's by a relative error of at most 0.0029.
Values sent between devices are 32-bit elements; how exact they have to be, the bound alone decides.
No kernel may reach another device: no remote copies, remote signals or barrier semaphores. Data moves between devices by JAX's collectives and lax.ppermute only.
A program may use at most 64 MiB of HBM per device.

v0:
```python
import jax
import jax.numpy as jnp
from jax import lax
from jax.sharding import PartitionSpec as P

BS = 32


DT = 0.2


def padded_2(block, sides, width):
    for axis, dim in sides:
        count = lax.axis_size(axis)
        forward = [(i, i + 1) for i in range(count - 1)]
        backward = [(target, source) for source, target in forward]
        low = lax.ppermute(
            lax.slice_in_dim(block, block.shape[dim] - width, None, axis=dim), axis, forward
        )
        high = lax.ppermute(lax.slice_in_dim(block, 0, width, axis=dim), axis, backward)
        block = jnp.concatenate([low, block, high], axis=dim)
    return block


def laplace(padded):
    centre = padded[1:-1, 1:-1]
    return (
        padded[2:, 1:-1] + padded[:-2, 1:-1] + padded[1:-1, 2:] + padded[1:-1, :-2] - 4.0 * centre
    )


def step_once(field, coef):
    bordered = padded_2(field, (("row", 0), ("col", 1)), 1)
    return field + coef * laplace(bordered)


def on_device(
    adj_final, kappa, elev_early, elev_late, basis, basis_index, intersection_patch, owner_row
):
    coef_late = DT * kappa / (1.0 + elev_late * elev_late)
    coef_early = DT * kappa / (1.0 + elev_early * elev_early)
    adj_mid = step_once(adj_final, coef_late)
    adj_start = step_once(adj_mid, coef_early)
    grad_field = (DT * (adj_final + adj_mid)).astype(jnp.bfloat16)
    tile_rows, tile_cols = grad_field.shape
    blocks = grad_field.reshape(tile_rows // BS, BS, tile_cols // BS, BS).transpose(0, 2, 1, 3)
    blocks = blocks.reshape(-1, BS * BS)
    nblock = blocks.shape[0]
    table = basis[0, 0]
    nbasis = table.shape[0]
    products = jnp.einsum("bk,qkn->qbn", blocks, table, preferred_element_type=jnp.float32)
    index = basis_index[0, 0].reshape(nblock, -1)
    select = (index[:, :, None] == jnp.arange(nbasis, dtype=jnp.int32)).astype(jnp.float32)
    contrib = jnp.einsum("boq,qbn->bon", select, products, precision=lax.Precision.HIGHEST)
    contrib = contrib.reshape(-1, contrib.shape[-1])
    strip_rows = owner_row[0]
    n_row = lax.axis_size("row")
    owned_count = strip_rows.shape[0] // n_row
    dest_row = jnp.take(strip_rows, intersection_patch[0, 0])
    count = lax.axis_size("row") * owned_count
    inside = (dest_row >= 0) & (dest_row < count)
    segment = jnp.where(inside, dest_row, count)
    owned = lax.psum_scatter(
        jax.ops.segment_sum(contrib, segment, num_segments=count + 1)[:count],
        "row",
        scatter_dimension=0,
        tiled=True,
    )
    return (adj_start, owned[None])


def solution(mesh):
    return jax.shard_map(
        on_device,
        mesh=mesh,
        in_specs=(
            P(("mem", "row"), "col"),
            P(("mem", "row"), "col"),
            P(("mem", "row"), "col"),
            P(("mem", "row"), "col"),
            P(("mem", "row"), "col", None, None, None),
            P(("mem", "row"), "col", None),
            P(("mem", "row"), "col", None),
            P(("mem", "col"), None),
        ),
        out_specs=(P(("mem", "row"), "col"), P(("mem", "col"), "row", None)),
        check_vma=False,
    )
```

profile of v0, /device:TPU:2, one launch (start us, length us, event | category | flops | bytes accessed | tf_op | source)
XLA Modules:
  0.0 169.8 jit_solution(15520277962530658819)
XLA Ops:
  7.2 0.0 reduce-scatter.2.cloned.1.call-start
  7.3 0.9 fusion.22
  8.2 1.7 %collective-permute-start.1 = (f32[1,1024]{1,0:T(1,128)S(1)}, f32[1,1024]{1,0:T(1,128)S(1)}, u32[]{:S(2)}, u32[]{:S(2)}) collective-permute-start(f32[1,1024]{1,0:T(1,128)S(1)} %get-tuple-element.10), channel_id=1, source_target_pairs={{0,16},{16,32},{32,48},{48,64},{64,80},{80,96},{96,112},{112,128},... | collective-permute-start | bytes 12296 | tf_op jit(solution)/shard_map/ppermute | solution.py:17
  9.9 1.3 collective-permute-start
  11.2 0.7 compare_select_fusion
  11.9 3.4 %gather_fusion = s32[512]{0:T(512)S(1)} fusion(s32[2048]{0:T(1024)} %bitcast.21, s32[1024]{0:T(1024)S(1)} %pad_clamp_fusion), kind=kCustom, calls=%fused_computation | custom fusion | bytes 6144 | tf_op jit(solution)/shard_map/jit(_take)/gather | solution.py:59
  15.3 0.1 pad_maximum_fusion.21
  15.4 1.3 collective-permute-start.2
  16.7 5.2 %collective-permute-start.3 = (f32[130,1]{1,0:T(8,128)S(1)}, f32[130,1]{1,0:T(8,128)}, u32[]{:S(2)}, u32[]{:S(2)}) collective-permute-start(f32[130,1]{1,0:T(8,128)S(1)} %get-tuple-element.7), channel_id=1, source_target_pairs={{0,4},{4,8},{8,12},{1,5},{5,9},{9,13},{2,6},{6,10},{10,14},{3,7},{... | collective-permute-start | bytes 1568 | tf_op jit(solution)/shard_map/ppermute | solution.py:17
  21.9 0.5 broadcast.100
  22.4 0.7 reduce.3
  23.1 0.1 eq.15
  23.2 1.7 %multiply_convert_fusion = (bf16[128,1024]{1,0:T(8,128)(2,1)S(1)}, f32[128,1024]{1,0:T(8,128)S(1)}) fusion(f32[128,1024]{1,0:T(8,128)S(1)} %copy-done.1, f32[1,1024]{1,0:T(1,128)S(1)} %collective-permute-done, f32[1,1024]{1,0:T(1,128)S(1)} %collective-permute-done.1, f32[130,1]{1,0:T(8,128)} %collective-permute-done.3, ...), kind=kLoop, calls=%fused_computation.38 | loop fusion | flops 2883584 | bytes 2368528 | tf_op jit(solution)/shard_map/convert_element_type | solution.py:44
  24.9 1.7 %reshape.86 = bf16[4,32,32,32]{3,2,1,0:T(8,128)(2,1)} reshape(bf16[128,1024]{1,0:T(8,128)(2,1)S(1)} %get-tuple-element.2) | data formatting | bytes 524288 | tf_op jit(solution)/shard_map/reshape | solution.py:46
  26.7 2.6 %copy.17 = bf16[4,32,32,32]{3,1,2,0:T(8,128)(2,1)} copy(bf16[4,32,32,32]{3,2,1,0:T(8,128)(2,1)} %reshape.86) | data formatting | bytes 524288 | tf_op jit(solution)/shard_map/reshape | solution.py:46
  29.3 2.3 %reshape.105 = bf16[128,1024,1]{1,0,2:T(8,128)(2,1)S(1)} reshape(bf16[4,32,32,32]{3,2,1,0:T(8,128)(2,1)} %bitcast.22) | data formatting | bytes 524288 | tf_op jit(solution)/shard_map/reshape | solution.py:47
  31.7 0.4 fusion
  32.1 0.9 fusion.16
  33.1 1.0 reshape.101
  34.0 5.2 %scatter_custom_fusion = f32[2049,256]{1,0:T(8,128)} fusion(s32[512]{0:T(512)S(1)} %bitcast.25, f32[512,256]{1,0:T(8,128)} %reshape.101, f32[]{:T(128)} %constant.11.clone.1), kind=kCustom, calls=%fused_computation.4 | custom fusion | flops 131072 | bytes 2098688 | tf_op jit(solution)/shard_map/scatter-add | solution.py:64
  39.2 3.0 %slice.80 = f32[2048,256]{1,0:T(8,128)} slice(f32[2049,256]{1,0:T(8,128)} %scatter_custom_fusion), slice={[0:2048], [0:256]} | slice | bytes 4194304 | tf_op jit(solution)/shard_map/slice | solution.py:64
  42.3 0.0 reduce-scatter.2.cloned.1.call-update
  42.3 4.3 %collective-permute-start.5 = (f32[1,1024]{1,0:T(1,128)S(1)}, f32[1,1024]{1,0:T(1,128)S(1)}, u32[]{:S(2)}, u32[]{:S(2)}) collective-permute-start(f32[1,1024]{1,0:T(1,128)S(1)} %get-tuple-element.8), channel_id=1, source_target_pairs={{0,16},{16,32},{32,48},{48,64},{64,80},{80,96},{96,112},{112,128},... | collective-permute-start | bytes 12296 | tf_op jit(solution)/shard_map/ppermute | solution.py:17
  46.6 1.3 collective-permute-start.4
  47.9 3.5 %collective-permute-done.4 = f32[1,1024]{1,0:T(1,128)S(1)} collective-permute-done((f32[1,1024]{1,0:T(1,128)S(1)}, f32[1,1024]{1,0:T(1,128)S(1)}, u32[]{:S(2)}, u32[]{:S(2)}) %collective-permute-start.4) | collective-permute-done | bytes 4128 | tf_op jit(solution)/shard_map/ppermute | solution.py:20
  51.5 0.1 pad_maximum_fusion.18
  51.6 1.3 collective-permute-start.6
  52.9 5.0 %collective-permute-start.7 = (f32[130,1]{1,0:T(8,128)S(1)}, f32[130,1]{1,0:T(8,128)S(1)}, u32[]{:S(2)}, u32[]{:S(2)}) collective-permute-start(f32[130,1]{1,0:T(8,128)S(1)} %get-tuple-element.5), channel_id=1, source_target_pairs={{0,4},{4,8},{8,12},{1,5},{5,9},{9,13},{2,6},{6,10},{10,14},{3,7},{... | collective-permute-start | bytes 1568 | tf_op jit(solution)/shard_map/ppermute | solution.py:17
  57.9 0.3 collective-permute-done.6
  58.2 1.6 collective-permute-done.7
  59.8 2.3 %fusion.7 = f32[128,1024]{1,0:T(8,128)} fusion(f32[128,1024]{1,0:T(8,128)S(1)} %get-tuple-element.3, f32[130,1]{1,0:T(8,128)S(1)} %collective-permute-done.7, f32[1,1024]{1,0:T(1,128)S(1)} %collective-permute-done.4, f32[1,1024]{1,0:T(1,128)S(1)} %collective-permute-done.5, f32[130,1]{1,0:T(8,128)S(1)} %collective-permute-done.6, f32[128,1024]{1,0:T(8,128)} %param.10, ...), kind=kLoop, calls=%fused_computation.11 | loop fusion | flops 2490368 | bytes 2106384 | tf_op jit(solution)/shard_map/add | solution.py:34
  62.1 100.9 %reduce-scatter.2.cloned.1.call-done = f32[64,256]{1,0:T(8,128)} async-done(((f32[2048,256]{1,0:T(8,128)}), f32[64,256]{1,0:T(8,128)}) %reduce-scatter.2.cloned.1.call-update) | async-done | bytes 65552 | tf_op jit(solution)/shard_map/reduce_scatter | solution.py:63
  (18 shorter events, 0.1 us)
Async XLA Ops:
  7.2 24.5 %copy-start = (bf16[1,1,4,1024,256]{4,3,2,1,0:T(8,128)(2,1)S(1)}, bf16[1,1,4,1024,256]{4,3,2,1,0:T(8,128)(2,1)}, u32[]{:S(2)}) copy-start(bf16[1,1,4,1024,256]{4,3,2,1,0:T(8,128)(2,1)} %param.12) | copy-start | bytes 6291460
  7.2 8.1 %copy-start.1 = (f32[128,1024]{1,0:T(8,128)S(1)}, f32[128,1024]{1,0:T(8,128)}, u32[]{:S(2)}) copy-start(f32[128,1024]{1,0:T(8,128)} %param.8) | copy-start | bytes 1572868
  7.2 14.7 %copy-start.3 = (s32[1,1,512]{2,1,0:T(1,128)S(1)}, s32[1,1,512]{2,1,0:T(1,128)}, u32[]{:S(2)}) copy-start(s32[1,1,512]{2,1,0:T(1,128)} %param.14) | copy-start | bytes 6148
  7.2 15.2 %copy-start.4 = (s32[1,1,512]{2,1,0:T(1,128)S(1)}, s32[1,1,512]{2,1,0:T(1,128)}, u32[]{:S(2)}) copy-start(s32[1,1,512]{2,1,0:T(1,128)} %param.13) | copy-start | bytes 6148
  7.2 155.8 %reduce-scatter.2.cloned.1.call-start = ((), (), s32[]{:S(2)}) async-start(), calls=%async_computation.1 | async-start | bytes 2162688 | tf_op jit(solution)/shard_map/reduce_scatter | solution.py:63
  8.2 7.1 %collective-permute-start.1 = (f32[1,1024]{1,0:T(1,128)S(1)}, f32[1,1024]{1,0:T(1,128)S(1)}, u32[]{:S(2)}, u32[]{:S(2)}) collective-permute-start(f32[1,1024]{1,0:T(1,128)S(1)} %get-tuple-element.10), channel_id=1, source_target_pairs={{0,16},{16,32},{32,48},{48,64},{64,80},{80,96},{96,112},{112,128},... | collective-permute-start | bytes 12296 | tf_op jit(solution)/shard_map/ppermute | solution.py:17
  9.9 5.4 %collective-permute-start = (f32[1,1024]{1,0:T(1,128)S(1)}, f32[1,1024]{1,0:T(1,128)S(1)}, u32[]{:S(2)}, u32[]{:S(2)}) collective-permute-start(f32[1,1024]{1,0:T(1,128)S(1)} %get-tuple-element.11), channel_id=1, source_target_pairs={{16,0},{32,16},{48,32},{64,48},{80,64},{96,80},{112,96},{128,112},... | collective-permute-start | bytes 12296 | tf_op jit(solution)/shard_map/ppermute | solution.py:20
  15.4 7.8 %collective-permute-start.2 = (f32[130,1]{1,0:T(8,128)S(1)}, f32[130,1]{1,0:T(8,128)S(1)}, u32[]{:S(2)}, u32[]{:S(2)}) collective-permute-start(f32[130,1]{1,0:T(8,128)S(1)} %get-tuple-element.6), channel_id=1, source_target_pairs={{4,0},{8,4},{12,8},{5,1},{9,5},{13,9},{6,2},{10,6},{14,10},{7,3},{... | collective-permute-start | bytes 1568 | tf_op jit(solution)/shard_map/ppermute | solution.py:20
  16.7 6.5 %collective-permute-start.3 = (f32[130,1]{1,0:T(8,128)S(1)}, f32[130,1]{1,0:T(8,128)}, u32[]{:S(2)}, u32[]{:S(2)}) collective-permute-start(f32[130,1]{1,0:T(8,128)S(1)} %get-tuple-element.7), channel_id=1, source_target_pairs={{0,4},{4,8},{8,12},{1,5},{5,9},{9,13},{2,6},{6,10},{10,14},{3,7},{... | collective-permute-start | bytes 1568 | tf_op jit(solution)/shard_map/ppermute | solution.py:17
  42.3 17.5 %copy-start.2 = (f32[128,1024]{1,0:T(8,128)S(1)}, f32[128,1024]{1,0:T(8,128)}, u32[]{:S(2)}) copy-start(f32[128,1024]{1,0:T(8,128)} %param.9) | copy-start | bytes 1572868
  42.3 5.6 %collective-permute-start.5 = (f32[1,1024]{1,0:T(1,128)S(1)}, f32[1,1024]{1,0:T(1,128)S(1)}, u32[]{:S(2)}, u32[]{:S(2)}) collective-permute-start(f32[1,1024]{1,0:T(1,128)S(1)} %get-tuple-element.8), channel_id=1, source_target_pairs={{0,16},{16,32},{32,48},{48,64},{64,80},{80,96},{96,112},{112,128},... | collective-permute-start | bytes 12296 | tf_op jit(solution)/shard_map/ppermute | solution.py:17
  46.6 4.9 %collective-permute-start.4 = (f32[1,1024]{1,0:T(1,128)S(1)}, f32[1,1024]{1,0:T(1,128)S(1)}, u32[]{:S(2)}, u32[]{:S(2)}) collective-permute-start(f32[1,1024]{1,0:T(1,128)S(1)} %get-tuple-element.9), channel_id=1, source_target_pairs={{16,0},{32,16},{48,32},{64,48},{80,64},{96,80},{112,96},{128,112},... | collective-permute-start | bytes 12296 | tf_op jit(solution)/shard_map/ppermute | solution.py:20
  51.6 6.6 %collective-permute-start.6 = (f32[130,1]{1,0:T(8,128)S(1)}, f32[130,1]{1,0:T(8,128)S(1)}, u32[]{:S(2)}, u32[]{:S(2)}) collective-permute-start(f32[130,1]{1,0:T(8,128)S(1)} %get-tuple-element.4), channel_id=1, source_target_pairs={{4,0},{8,4},{12,8},{5,1},{9,5},{13,9},{6,2},{10,6},{14,10},{7,3},{... | collective-permute-start | bytes 1568 | tf_op jit(solution)/shard_map/ppermute | solution.py:20
  52.9 6.9 %collective-permute-start.7 = (f32[130,1]{1,0:T(8,128)S(1)}, f32[130,1]{1,0:T(8,128)S(1)}, u32[]{:S(2)}, u32[]{:S(2)}) collective-permute-start(f32[130,1]{1,0:T(8,128)S(1)} %get-tuple-element.5), channel_id=1, source_target_pairs={{0,4},{4,8},{8,12},{1,5},{5,9},{9,13},{2,6},{6,10},{10,14},{3,7},{... | collective-permute-start | bytes 1568 | tf_op jit(solution)/shard_map/ppermute | solution.py:17
Sparse Core Ops, SparseCore 0:
  42.4 120.5 reduce-scatter.1
where the time goes:
time: 170 us
  waiting for transfers between devices  106 us (62%)
  starting transfers between devices  21.4 us (13%)
  local copies, waits for them, and re-layouts  15.7 us (9%)
  between operations  14.2 us (8%)
  other arithmetic  10.8 us (6%)
    reduce_scatter x1, waiting for transfers between devices, on_device(): lax.psum_scatter(jax.ops.segment_sum(contrib, segment, num_segments=count...  101 us
    ppermute x4, starting transfers between devices, padded_2(): lax.ppermute(lax.slice_in_dim(block, block.shape[dim] - width, None, axis...  16.2 us
    scatter-add x1, other arithmetic, on_device(): jax.ops.segment_sum(contrib, segment, num_segments=count + 1)[:count]  5.21 us
    ppermute x4, starting transfers between devices, padded_2(): lax.ppermute(lax.slice_in_dim(block, 0, width, axis=dim), axis, backward)  5.17 us
    reshape x2, local copies, waits for them, and re-layouts, on_device(): grad_field.reshape(tile_rows // BS, BS, tile_cols // BS, BS)  4.38 us
    ppermute x4, waiting for transfers between devices, padded_2(): lax.ppermute(lax.slice_in_dim(block, 0, width, axis=dim), axis, backward)  3.9 us
  transfers between devices with their start and end apart: 9, of which 4 were waited for; matrix products, arithmetic and copies ran while one was open for 5% of the time, Pallas kernels for 0%

commit v1 on v0

v1 whole, which is shorter than its diff:
```python
import functools

import jax
import jax.numpy as jnp
from jax import lax
from jax.experimental import pallas as pl
from jax.experimental.pallas import tpu as pltpu
from jax.sharding import PartitionSpec as P

BS = 32
DT = 0.2
F32 = jnp.float32
BF16 = jnp.bfloat16
I32 = jnp.int32
VLIM = 24 << 20


def whole(shape):
    return jax.ShapeDtypeStruct(shape, F32)


def vmem():
    return pl.BlockSpec(memory_space=pltpu.VMEM)


def params(limit=VLIM):
    return pltpu.CompilerParams(vmem_limit_bytes=limit)


def edges_kernel(top_ref, bot_ref, left_ref, right_ref, t_ref, b_ref, l_ref, r_ref):
    t_ref[...] = top_ref[0:1, :]
    b_ref[...] = bot_ref[7:8, :]
    l_ref[...] = left_ref[...].T[0:1, :]
    r_ref[...] = right_ref[...].T[127:128, :]


def edges(a):
    rows, cols = a.shape
    return pl.pallas_call(
        edges_kernel,
        grid=(1,),
        in_specs=[
            pl.BlockSpec((8, cols), lambda i: (0, 0)),
            pl.BlockSpec((8, cols), lambda i: (rows // 8 - 1, 0)),
            pl.BlockSpec((rows, 128), lambda i: (0, 0)),
            pl.BlockSpec((rows, 128), lambda i: (0, cols // 128 - 1)),
        ],
        out_specs=[
            pl.BlockSpec((1, cols), lambda i: (0, 0)),
            pl.BlockSpec((1, cols), lambda i: (0, 0)),
            pl.BlockSpec((1, rows), lambda i: (0, 0)),
            pl.BlockSpec((1, rows), lambda i: (0, 0)),
        ],
        out_shape=[whole((1, cols)), whole((1, cols)), whole((1, rows)), whole((1, rows))],
        compiler_params=params(4 << 20),
        name="edges",
    )(a, a, a, a)


def index_kernel(core_ref, patch_ref, owner_ref, idx_ref, dest_ref, sel_ref):
    entries = patch_ref.shape[1]
    patches = owner_ref.shape[1]
    hot = lax.broadcasted_iota(I32, (patches, entries), 0) == patch_ref[...]
    hot = jnp.where(hot, 1.0, 0.0).astype(BF16)
    owner = owner_ref[...]
    row = lax.broadcasted_iota(I32, (16, patches), 0)
    parts = jnp.where(row == 0, owner >> 6, jnp.where(row == 1, owner & 63, 0))
    found = jnp.dot(parts.astype(F32).astype(BF16), hot, preferred_element_type=F32)
    high = found[0:1, :].astype(I32) ^ core_ref[0]
    low = found[1:2, :].astype(I32)
    spot = jnp.zeros_like(high)
    for bit in range(5):
        spot = spot | (((high >> bit) & 1) << (4 - bit))
    dest_ref[...] = spot * 64 + low
    nb = entries // 4
    lane = lax.broadcasted_iota(I32, (nb, entries), 1)
    block = lax.broadcasted_iota(I32, (nb, entries), 0)
    idx = jnp.broadcast_to(idx_ref[...], (nb, entries))
    for o in range(4):
        sel_ref[:, o : o + 1] = jnp.sum(
            jnp.where(lane == block * 4 + o, idx, 0), axis=1, keepdims=True
        )


def indices(core, patch, owner, idx):
    entries = patch.shape[1]
    return pl.pallas_call(
        index_kernel,
        in_specs=[pl.BlockSpec(memory_space=pltpu.SMEM), vmem(), vmem(), vmem()],
        out_specs=[vmem(), vmem()],
        out_shape=[
            jax.ShapeDtypeStruct((1, entries), I32),
            jax.ShapeDtypeStruct((entries // 4, 4), I32),
        ],
        compiler_params=params(),
        name="indices",
    )(core, patch, owner, idx)


def stencil(a_ref, kap_ref, elev_ref, n_ref, s_ref, wt, et, emit):
    rows, cols = a_ref.shape
    lane = lax.broadcasted_iota(I32, (8, cols), 1)
    sub = lax.broadcasted_iota(I32, (8, cols), 0)
    for i in range(rows // 8):
        r = 8 * i
        x = a_ref[r : r + 8, :]
        if i == 0:
            up = jnp.where(sub == 0, n_ref[...], pltpu.roll(x, 1, 0))
        else:
            up = a_ref[r - 1 : r + 7, :]
        if i == rows // 8 - 1:
            down = jnp.where(sub == 7, s_ref[...], pltpu.roll(x, 7, 0))
        else:
            down = a_ref[r + 1 : r + 9, :]
        east = jnp.where(lane == cols - 1, et[r : r + 8, 0:1], pltpu.roll(x, cols - 1, 1))
        west = jnp.where(lane == 0, wt[r : r + 8, 0:1], pltpu.roll(x, 1, 1))
        e = elev_ref[r : r + 8, :]
        coef = DT * kap_ref[r : r + 8, :] / (1.0 + e * e)
        lap = down + up + east + west - 4.0 * x
        emit(r, x, x + coef * lap)


def column(ref):
    n = ref.shape[1]
    return jnp.broadcast_to(ref[...], (128, n)).T


def hot_rows(dest, start, count):
    entries = dest.shape[1]
    row = lax.broadcasted_iota(I32, (count, entries), 0) + start
    return jnp.where(row == dest, 1.0, 0.0).astype(BF16)


def gather_rows(out_ref, dest, hi, lo, first):
    rows = out_ref.shape[0]
    step = 256
    for k in range(rows // step):
        hot = hot_rows(dest, first + k * step, step)
        total = jnp.dot(hot, hi, preferred_element_type=F32)
        total += jnp.dot(hot, lo, preferred_element_type=F32)
        out_ref[k * step : (k + 1) * step, :] = total


def main_kernel(
    a_ref, kap_ref, elev_ref, n_ref, s_ref, w_ref, e_ref, basis_ref, dest_ref, sel_ref,
    mid_ref, t_ref, b_ref, l_ref, r_ref, hi_ref, lo_ref, send_ref,
    wt, et, g_ref, y_ref, c_ref,
):
    rows, cols = a_ref.shape
    wt[...] = column(w_ref)
    et[...] = column(e_ref)

    def emit(r, x, mid):
        mid_ref[r : r + 8, :] = mid
        g = DT * (x + mid)
        for k in range(cols // 128):
            g_ref[k, r : r + 8, :] = g[:, k * 128 : (k + 1) * 128]

    stencil(a_ref, kap_ref, elev_ref, n_ref, s_ref, wt, et, emit)
    nb = rows * cols // (BS * BS)
    chunk = lax.broadcasted_iota(I32, (8, 128), 1) // BS
    for br in range(rows // BS):
        for bh in range(cols // 128):
            v = [
                g_ref[bh, pl.ds(br * BS + rl, 8, stride=4), :]
                for rl in range(4)
            ]
            for bl in range(4):
                out = v[bl]
                for rl in range(4):
                    if rl != bl:
                        moved = pltpu.roll(v[rl], ((rl - bl) * BS) % 128, 1)
                        out = jnp.where(chunk == rl, moved, out)
                b = br * (cols // BS) + bh * 4 + bl
                y_ref[pl.ds(b, 8, stride=nb), :] = out
    lhs = jnp.concatenate(
        [y_ref[rh * nb : (rh + 1) * nb, :].astype(BF16) for rh in range(8)], axis=1
    )
    products = [
        jnp.dot(lhs, basis_ref[q], preferred_element_type=F32)
        for q in range(basis_ref.shape[0])
    ]
    for o in range(4):
        sel = sel_ref[:, o : o + 1]
        out = jnp.zeros_like(products[0])
        for q, product in enumerate(products):
            out = jnp.where(sel == q, product, out)
        for h in range(2):
            c_ref[h, pl.ds(o, nb, stride=4), :] = out[:, h * 128 : (h + 1) * 128]
    contrib = jnp.concatenate([c_ref[0], c_ref[1]], axis=1)
    hi = contrib.astype(BF16)
    lo = (contrib - hi.astype(F32)).astype(BF16)
    hi_ref[...] = hi
    lo_ref[...] = lo
    gather_rows(send_ref, dest_ref[...], hi, lo, send_ref.shape[0])
    t_ref[...] = mid_ref[0:1, :]
    b_ref[...] = mid_ref[rows - 1 : rows, :]
    l_ref[...] = mid_ref[:, 0:128].T[0:1, :]
    r_ref[...] = mid_ref[:, cols - 128 : cols].T[127:128, :]


def main(a, kappa, elev, halo, basis, dest, sel, total):
    rows, cols = a.shape
    entries = dest.shape[1]
    ncoef = basis.shape[-1]
    return pl.pallas_call(
        main_kernel,
        in_specs=[vmem()] * 10,
        out_specs=[vmem()] * 8,
        out_shape=[
            whole((rows, cols)),
            whole((1, cols)),
            whole((1, cols)),
            whole((1, rows)),
            whole((1, rows)),
            jax.ShapeDtypeStruct((entries, ncoef), BF16),
            jax.ShapeDtypeStruct((entries, ncoef), BF16),
            whole((total // 2, ncoef)),
        ],
        scratch_shapes=[
            pltpu.VMEM((rows, 128), F32),
            pltpu.VMEM((rows, 128), F32),
            pltpu.VMEM((cols // 128, rows, 128), F32),
            pltpu.VMEM((rows * cols // 128, 128), F32),
            pltpu.VMEM((2, entries, 128), F32),
        ],
        compiler_params=params(),
        cost_estimate=pl.CostEstimate(
            flops=10**9, bytes_accessed=6 << 20, transcendentals=0
        ),
        name="main",
    )(a, kappa, elev, *halo, basis, dest, sel)


def keep_kernel(dest_ref, hi_ref, lo_ref, out_ref):
    gather_rows(out_ref, dest_ref[...], hi_ref[...], lo_ref[...], 0)


def keep_rows(dest, hi, lo, total):
    return pl.pallas_call(
        keep_kernel,
        in_specs=[vmem()] * 3,
        out_specs=vmem(),
        out_shape=whole((total // 2, hi.shape[1])),
        compiler_params=params(),
        cost_estimate=pl.CostEstimate(
            flops=5 * 10**8, bytes_accessed=1 << 20, transcendentals=0
        ),
        name="keep",
    )(dest, hi, lo)


def last_kernel(a_ref, kap_ref, elev_ref, n_ref, s_ref, w_ref, e_ref, out_ref, wt, et):
    wt[...] = column(w_ref)
    et[...] = column(e_ref)

    def emit(r, x, new):
        out_ref[r : r + 8, :] = new

    stencil(a_ref, kap_ref, elev_ref, n_ref, s_ref, wt, et, emit)


def last(a, kappa, elev, halo):
    rows, cols = a.shape
    return pl.pallas_call(
        last_kernel,
        in_specs=[vmem()] * 7,
        out_specs=vmem(),
        out_shape=whole((rows, cols)),
        scratch_shapes=[pltpu.VMEM((rows, 128), F32), pltpu.VMEM((rows, 128), F32)],
        compiler_params=params(),
        cost_estimate=pl.CostEstimate(
            flops=10**7, bytes_accessed=2 << 20, transcendentals=0
        ),
        name="last",
    )(a, kappa, elev, *halo)


def exchange(top, bottom, left, right):
    halo = []
    for axis, low, high in (("row", bottom, top), ("col", right, left)):
        count = lax.axis_size(axis)
        forward = [(i, i + 1) for i in range(count - 1)]
        backward = [(target, source) for source, target in forward]
        halo.append(lax.ppermute(low, axis, forward))
        halo.append(lax.ppermute(high, axis, backward))
    return halo


def partners(n_chip, distance):
    pairs = []
    for z in range(n_chip):
        for core in range(2):
            low = (z // distance) % 2 == core
            other = (z + (distance if low else -distance)) % n_chip
            pairs.append((2 * z + core, 2 * other + core))
    return pairs


def on_device(
    adj_final, kappa, elev_early, elev_late, basis, basis_index, intersection_patch, owner_row
):
    n_row = lax.axis_size("row")
    total = owner_row.shape[1]
    place = lax.axis_index("row").astype(I32)
    core, chip = place & 1, place >> 1
    halo = exchange(*edges(adj_final))
    dest, sel = indices(core.reshape(1), intersection_patch[0], owner_row, basis_index[0])
    mid, top, bottom, left, right, hi, lo, send = main(
        adj_final, kappa, elev_late, halo, basis[0, 0], dest, sel, total
    )
    got = lax.ppermute(send, "row", [(i, i ^ 1) for i in range(n_row)])
    part = keep_rows(dest, hi, lo, total) + got
    halo = exchange(top, bottom, left, right)
    adj_start = last(mid, kappa, elev_early, halo)
    distance = 1
    while distance < n_row // 2:
        half = part.shape[0] // 2
        upper = (chip // distance) & 1
        sent = lax.dynamic_slice_in_dim(part, (1 - upper) * half, half)
        got = lax.ppermute(sent, "row", partners(n_row // 2, distance))
        part = lax.dynamic_slice_in_dim(part, upper * half, half) + got
        distance *= 2
    return (adj_start, part[None])


def solution(mesh):
    return jax.shard_map(
        on_device,
        mesh=mesh,
        in_specs=(
            P(("mem", "row"), "col"),
            P(("mem", "row"), "col"),
            P(("mem", "row"), "col"),
            P(("mem", "row"), "col"),
            P(("mem", "row"), "col", None, None, None),
            P(("mem", "row"), "col", None),
            P(("mem", "row"), "col", None),
            P(("mem", "col"), None),
        ),
        out_specs=(P(("mem", "row"), "col"), P(("mem", "col"), "row", None)),
        check_vma=False,
    )
```

time: 170 us -> 97.8 us (0.58)
  the two profiles are of different devices: /device:TPU:2 before, /device:TPU:34 now
where the time goes in v1:
time: 97.8 us; the launch traced here: 97.2 us
  starting transfers between devices  54.7 us (56%)
  waiting for transfers between devices  28.8 us (29%)
  Pallas kernels  5.06 us (5%)
  local copies, waits for them, and re-layouts  4.4 us (4%)
  other arithmetic  3.16 us (3%)
  between operations  1.01 us (1%)
    ppermute x4, starting transfers between devices, on_device(): got = lax.ppermute(sent, 'row', partners(n_row // 2, distance))  32 us
    ppermute x4, waiting for transfers between devices, on_device(): got = lax.ppermute(sent, 'row', partners(n_row // 2, distance))  20.1 us
    ppermute x4, starting transfers between devices, exchange(): halo.append(lax.ppermute(low, axis, forward))  11 us
    ppermute x4, starting transfers between devices, exchange(): halo.append(lax.ppermute(high, axis, backward))  9.87 us
    ppermute x4, waiting for transfers between devices, exchange(): halo.append(lax.ppermute(high, axis, backward))  7.65 us
    unnamed x22, local copies, waits for them, and re-layouts  4.29 us
    pallas_call x1, Pallas kernels, main(): pl.pallas_call(main_kernel, in_specs=[vmem()] * 10, out_specs=[vmem()] *...  2.32 us
  transfers between devices with their start and end apart: 13, of which 6 were waited for; matrix products, arithmetic and copies ran while one was open for 0% of the time, Pallas kernels for 3%

profile of v1, /device:TPU:34, one launch (start us, length us, event | category | flops | bytes accessed | tf_op | source)
XLA Modules:
  0.0 97.2 jit_solution(5699342599452268984)
XLA Ops:
  0.6 1.0 %copy-done = f32[128,1024]{1,0:T(8,128)S(1)} copy-done((f32[128,1024]{1,0:T(8,128)S(1)}, f32[128,1024]{1,0:T(8,128)}, u32[]{:S(2)}) %copy-start) | copy-done | bytes 524312
  1.7 0.1 edges.1
  1.8 2.1 %collective-permute-start = (f32[1,1024]{1,0:T(1,128)S(1)}, f32[1,1024]{1,0:T(1,128)S(1)}, u32[]{:S(2)}, u32[]{:S(2)}) collective-permute-start(f32[1,1024]{1,0:T(1,128)S(1)} %get-tuple-element.16), channel_id=1, source_target_pairs={{0,16},{16,32},{32,48},{48,64},{64,80},{80,96},{96,112},{112,128},... | collective-permute-start | bytes 12296 | tf_op jit(solution)/shard_map/ppermute | solution.py:285
  3.9 3.6 %collective-permute-start.1 = (f32[1,1024]{1,0:T(1,128)S(1)}, f32[1,1024]{1,0:T(1,128)S(1)}, u32[]{:S(2)}, u32[]{:S(2)}) collective-permute-start(f32[1,1024]{1,0:T(1,128)S(1)} %get-tuple-element.17), channel_id=1, source_target_pairs={{16,0},{32,16},{48,32},{64,48},{80,64},{96,80},{112,96},{128,112},... | collective-permute-start | bytes 12296 | tf_op jit(solution)/shard_map/ppermute | solution.py:286
  7.5 3.5 %collective-permute-start.2 = (f32[1,128]{1,0:T(1,128)S(1)}, f32[1,128]{1,0:T(1,128)S(1)}, u32[]{:S(2)}, u32[]{:S(2)}) collective-permute-start(f32[1,128]{1,0:T(1,128)S(1)} %get-tuple-element.18), channel_id=1, source_target_pairs={{0,4},{4,8},{8,12},{1,5},{5,9},{9,13},{2,6},{6,10},{10,14},{3,7},{... | collective-permute-start | bytes 1544 | tf_op jit(solution)/shard_map/ppermute | solution.py:285
  11.0 1.3 %collective-permute-start.3 = (f32[1,128]{1,0:T(1,128)S(1)}, f32[1,128]{1,0:T(1,128)S(1)}, u32[]{:S(2)}, u32[]{:S(2)}) collective-permute-start(f32[1,128]{1,0:T(1,128)S(1)} %get-tuple-element.19), channel_id=1, source_target_pairs={{4,0},{8,4},{12,8},{5,1},{9,5},{13,9},{6,2},{10,6},{14,10},{7,3},{... | collective-permute-start | bytes 1544 | tf_op jit(solution)/shard_map/ppermute | solution.py:286
  12.3 0.6 indices.1
  13.0 3.5 %collective-permute-done.3.e_ref = f32[1,128]{1,0:T(1,128)S(1)} collective-permute-done((f32[1,128]{1,0:T(1,128)S(1)}, f32[1,128]{1,0:T(1,128)S(1)}, u32[]{:S(2)}, u32[]{:S(2)}) %collective-permute-start.3) | collective-permute-done | bytes 544 | tf_op jit(solution)/shard_map/ppermute | solution.py:286
  16.5 1.6 %copy-done.2 = bf16[1,1,4,1024,256]{4,3,2,1,0:T(8,128)(2,1)S(1)} copy-done((bf16[1,1,4,1024,256]{4,3,2,1,0:T(8,128)(2,1)S(1)}, bf16[1,1,4,1024,256]{4,3,2,1,0:T(8,128)(2,1)}, u32[]{:S(2)}) %copy-start.2) | copy-done | bytes 2097176
  18.1 2.3 %main.1 = (f32[128,1024]{1,0:T(8,128)S(1)}, f32[1,1024]{1,0:T(1,128)S(1)}, f32[1,1024]{1,0:T(1,128)S(1)}, f32[1,128]{1,0:T(1,128)S(1)}, f32[1,128]{1,0:T(1,128)S...) custom-call(f32[128,1024]{1,0:T(8,128)S(1)} %copy-done.1, ...), custom_call_target="tpu_custom_call" | custom-call | flops 1000000000 | bytes 6291456 | tf_op jit(solution)/shard_map/main/pallas_call | solution.py:206
  20.4 0.7 copy-done.9
  21.1 1.9 %collective-permute-start.8 = (f32[1024,256]{1,0:T(8,128)S(1)}, f32[1024,256]{1,0:T(8,128)}, u32[]{:S(2)}, u32[]{:S(2)}) collective-permute-start(f32[1024,256]{1,0:T(8,128)S(1)} %get-tuple-element.29), channel_id=1, source_target_pairs={{0,16},{16,0},{32,48},{48,32},{64,80},{80,64},{96,112},{112,96},{1... | collective-permute-start | bytes 3145736 | tf_op jit(solution)/shard_map/ppermute | solution.py:312
  23.1 0.9 copy-done.10
  24.0 0.7 keep.1
  24.7 1.1 %collective-permute-done.8 = f32[1024,256]{1,0:T(8,128)} collective-permute-done((f32[1024,256]{1,0:T(8,128)S(1)}, f32[1024,256]{1,0:T(8,128)}, u32[]{:S(2)}, u32[]{:S(2)}) %collective-permute-start.8) | collective-permute-done | bytes 1048608 | tf_op jit(solution)/shard_map/ppermute | solution.py:312
  25.8 1.4 %add.43 = f32[1024,256]{1,0:T(8,128)S(1)} add(f32[1024,256]{1,0:T(8,128)S(1)} %keep.1, f32[1024,256]{1,0:T(8,128)} %collective-permute-done.8) | non-fusion elementwise | flops 262144 | bytes 3145728 | tf_op jit(solution)/shard_map/add | solution.py:313
  27.2 0.0 copy-start.5
  27.2 2.1 %collective-permute-start.9 = (f32[512,256]{1,0:T(8,128)S(1)}, f32[512,256]{1,0:T(8,128)}, u32[]{:S(2)}, u32[]{:S(2)}) collective-permute-start(f32[512,256]{1,0:T(8,128)S(1)} %constant_dynamic-slice_fusion.3), channel_id=1, source_target_pairs={{0,32},{16,496},{32,0},{48,80},{64,96},{80,48},{96,64},{112,144},{... | collective-permute-start | bytes 1572872 | tf_op jit(solution)/shard_map/ppermute | solution.py:321
  29.3 9.2 %collective-permute-done.9 = f32[512,256]{1,0:T(8,128)} collective-permute-done((f32[512,256]{1,0:T(8,128)S(1)}, f32[512,256]{1,0:T(8,128)}, u32[]{:S(2)}, u32[]{:S(2)}) %collective-permute-start.9) | collective-permute-done | bytes 524320 | tf_op jit(solution)/shard_map/ppermute | solution.py:321
  38.5 1.1 %dynamic-slice_add_fusion = f32[512,256]{1,0:T(8,128)S(1)} fusion(f32[512,256]{1,0:T(8,128)} %collective-permute-done.9, f32[1024,256]{1,0:T(8,128)S(1)} %add.43, s32[]{:T(128)S(6)} %select_n.36), kind=kLoop, calls=%fused_computation | loop fusion | flops 131072 | bytes 1572868 | tf_op jit(solution)/shard_map/add | solution.py:322
  39.7 5.2 %collective-permute-start.10 = (f32[256,256]{1,0:T(8,128)S(1)}, f32[256,256]{1,0:T(8,128)S(1)}, u32[]{:S(2)}, u32[]{:S(2)}) collective-permute-start(f32[256,256]{1,0:T(8,128)S(1)} %constant_dynamic-slice_fusion.2), channel_id=1, source_target_pairs={{0,64},{16,464},{32,96},{48,496},{64,0},{80,144},{96,32},{112,176}... | collective-permute-start | bytes 786440 | tf_op jit(solution)/shard_map/ppermute | solution.py:321
  44.9 6.3 %collective-permute-done.10 = f32[256,256]{1,0:T(8,128)S(1)} collective-permute-done((f32[256,256]{1,0:T(8,128)S(1)}, f32[256,256]{1,0:T(8,128)S(1)}, u32[]{:S(2)}, u32[]{:S(2)}) %collective-permute-start.10) | collective-permute-done | bytes 262176 | tf_op jit(solution)/shard_map/ppermute | solution.py:321
  51.2 9.5 %collective-permute-start.11 = (f32[128,256]{1,0:T(8,128)S(1)}, f32[128,256]{1,0:T(8,128)S(1)}, u32[]{:S(2)}, u32[]{:S(2)}) collective-permute-start(f32[128,256]{1,0:T(8,128)S(1)} %constant_dynamic-slice_fusion.1), channel_id=1, source_target_pairs={{0,128},{16,400},{32,160},{48,432},{64,192},{80,464},{96,224},{112... | collective-permute-start | bytes 393224 | tf_op jit(solution)/shard_map/ppermute | solution.py:321
  60.7 4.6 %collective-permute-done.11 = f32[128,256]{1,0:T(8,128)S(1)} collective-permute-done((f32[128,256]{1,0:T(8,128)S(1)}, f32[128,256]{1,0:T(8,128)S(1)}, u32[]{:S(2)}, u32[]{:S(2)}) %collective-permute-start.11) | collective-permute-done | bytes 131104 | tf_op jit(solution)/shard_map/ppermute | solution.py:321
  65.4 15.2 %collective-permute-start.12 = (f32[64,256]{1,0:T(8,128)S(1)}, f32[64,256]{1,0:T(8,128)S(1)}, u32[]{:S(2)}, u32[]{:S(2)}) collective-permute-start(f32[64,256]{1,0:T(8,128)S(1)} %constant_dynamic-slice_fusion), channel_id=1, source_target_pairs={{0,256},{16,272},{32,288},{48,304},{64,320},{80,336},{96,352},{112... | collective-permute-start | bytes 196616 | tf_op jit(solution)/shard_map/ppermute | solution.py:321
  80.6 1.9 %collective-permute-start.4 = (f32[1,1024]{1,0:T(1,128)S(1)}, f32[1,1024]{1,0:T(1,128)S(1)}, u32[]{:S(2)}, u32[]{:S(2)}) collective-permute-start(f32[1,1024]{1,0:T(1,128)S(1)} %get-tuple-element.23), channel_id=1, source_target_pairs={{0,16},{16,32},{32,48},{48,64},{64,80},{80,96},{96,112},{112,128},... | collective-permute-start | bytes 12296 | tf_op jit(solution)/shard_map/ppermute | solution.py:285
  82.6 3.6 %collective-permute-start.5 = (f32[1,1024]{1,0:T(1,128)S(1)}, f32[1,1024]{1,0:T(1,128)S(1)}, u32[]{:S(2)}, u32[]{:S(2)}) collective-permute-start(f32[1,1024]{1,0:T(1,128)S(1)} %get-tuple-element.24), channel_id=1, source_target_pairs={{16,0},{32,16},{48,32},{64,48},{80,64},{96,80},{112,96},{128,112},... | collective-permute-start | bytes 12296 | tf_op jit(solution)/shard_map/ppermute | solution.py:286
  86.2 3.5 %collective-permute-start.6 = (f32[1,128]{1,0:T(1,128)S(1)}, f32[1,128]{1,0:T(1,128)S(1)}, u32[]{:S(2)}, u32[]{:S(2)}) collective-permute-start(f32[1,128]{1,0:T(1,128)S(1)} %get-tuple-element.25), channel_id=1, source_target_pairs={{0,4},{4,8},{8,12},{1,5},{5,9},{9,13},{2,6},{6,10},{10,14},{3,7},{... | collective-permute-start | bytes 1544 | tf_op jit(solution)/shard_map/ppermute | solution.py:285
  89.7 1.3 %collective-permute-start.7 = (f32[1,128]{1,0:T(1,128)S(1)}, f32[1,128]{1,0:T(1,128)S(1)}, u32[]{:S(2)}, u32[]{:S(2)}) collective-permute-start(f32[1,128]{1,0:T(1,128)S(1)} %get-tuple-element.26), channel_id=1, source_target_pairs={{4,0},{8,4},{12,8},{5,1},{9,5},{13,9},{6,2},{10,6},{14,10},{7,3},{... | collective-permute-start | bytes 1544 | tf_op jit(solution)/shard_map/ppermute | solution.py:286
  91.0 4.1 %collective-permute-done.7.e_ref = f32[1,128]{1,0:T(1,128)S(1)} collective-permute-done((f32[1,128]{1,0:T(1,128)S(1)}, f32[1,128]{1,0:T(1,128)S(1)}, u32[]{:S(2)}, u32[]{:S(2)}) %collective-permute-start.7) | collective-permute-done | bytes 544 | tf_op jit(solution)/shard_map/ppermute | solution.py:286
  95.2 1.3 %last.1 = f32[128,1024]{1,0:T(8,128)} custom-call(f32[128,1024]{1,0:T(8,128)S(1)} %get-tuple-element.22.a_ref, f32[128,1024]{1,0:T(8,128)S(1)} %copy-done.3, f32[128,1024]{1,0:T(8,128)S(1)} %copy-done.5, f32[1,1024]{1,0:T(1,128)S(1)} %collective-permute-done.4.n_ref, f32[1,1024]{1,0:T(1,128)S(1)} %collective-permute-done.5.s_ref, ...), custom_call_target="tpu_custom_call" | custom-call | flops 10000000 | bytes 2097152 | tf_op jit(solution)/shard_map/last/pallas_call | solution.py:265
  96.5 0.6 add_bitcast_fusion
  (30 shorter events, 0.2 us)
Async XLA Ops:
  0.6 1.0 %copy-start = (f32[128,1024]{1,0:T(8,128)S(1)}, f32[128,1024]{1,0:T(8,128)}, u32[]{:S(2)}) copy-start(f32[128,1024]{1,0:T(8,128)} %a_ref.1) | copy-start | bytes 1572868
  1.7 10.6 %copy-start.6 = (s32[1,2048]{1,0:T(1,128)S(1)}, s32[1,2048]{1,0:T(1,128)}, u32[]{:S(2)}) copy-start(s32[1,2048]{1,0:T(1,128)} %owner_ref.1) | copy-start | bytes 24580
  1.7 10.6 %copy-start.7 = (s32[1,1,512]{2,1,0:T(1,128)S(1)}, s32[1,1,512]{2,1,0:T(1,128)}, u32[]{:S(2)}) copy-start(s32[1,1,512]{2,1,0:T(1,128)} %param.14) | copy-start | bytes 6148
  1.7 10.6 %copy-start.8 = (s32[1,1,512]{2,1,0:T(1,128)S(1)}, s32[1,1,512]{2,1,0:T(1,128)}, u32[]{:S(2)}) copy-start(s32[1,1,512]{2,1,0:T(1,128)} %param.13) | copy-start | bytes 6148
  1.7 14.8 %copy-start.1 = (f32[128,1024]{1,0:T(8,128)S(1)}, f32[128,1024]{1,0:T(8,128)}, u32[]{:S(2)}) copy-start(f32[128,1024]{1,0:T(8,128)} %a_ref.1) | copy-start | bytes 1572868
  1.7 14.8 %copy-start.3 = (f32[128,1024]{1,0:T(8,128)S(1)}, f32[128,1024]{1,0:T(8,128)}, u32[]{:S(2)}) copy-start(f32[128,1024]{1,0:T(8,128)} %kap_ref.3) | copy-start | bytes 1572868
  1.7 14.8 %copy-start.4 = (f32[128,1024]{1,0:T(8,128)S(1)}, f32[128,1024]{1,0:T(8,128)}, u32[]{:S(2)}) copy-start(f32[128,1024]{1,0:T(8,128)} %elev_ref.2) | copy-start | bytes 1572868
  1.8 14.7 %collective-permute-start = (f32[1,1024]{1,0:T(1,128)S(1)}, f32[1,1024]{1,0:T(1,128)S(1)}, u32[]{:S(2)}, u32[]{:S(2)}) collective-permute-start(f32[1,1024]{1,0:T(1,128)S(1)} %get-tuple-element.16), channel_id=1, source_target_pairs={{0,16},{16,32},{32,48},{48,64},{64,80},{80,96},{96,112},{112,128},... | collective-permute-start | bytes 12296 | tf_op jit(solution)/shard_map/ppermute | solution.py:285
  3.9 12.6 %collective-permute-start.1 = (f32[1,1024]{1,0:T(1,128)S(1)}, f32[1,1024]{1,0:T(1,128)S(1)}, u32[]{:S(2)}, u32[]{:S(2)}) collective-permute-start(f32[1,1024]{1,0:T(1,128)S(1)} %get-tuple-element.17), channel_id=1, source_target_pairs={{16,0},{32,16},{48,32},{64,48},{80,64},{96,80},{112,96},{128,112},... | collective-permute-start | bytes 12296 | tf_op jit(solution)/shard_map/ppermute | solution.py:286
  7.5 5.5 %collective-permute-start.2 = (f32[1,128]{1,0:T(1,128)S(1)}, f32[1,128]{1,0:T(1,128)S(1)}, u32[]{:S(2)}, u32[]{:S(2)}) collective-permute-start(f32[1,128]{1,0:T(1,128)S(1)} %get-tuple-element.18), channel_id=1, source_target_pairs={{0,4},{4,8},{8,12},{1,5},{5,9},{9,13},{2,6},{6,10},{10,14},{3,7},{... | collective-permute-start | bytes 1544 | tf_op jit(solution)/shard_map/ppermute | solution.py:285
  11.0 5.5 %collective-permute-start.3 = (f32[1,128]{1,0:T(1,128)S(1)}, f32[1,128]{1,0:T(1,128)S(1)}, u32[]{:S(2)}, u32[]{:S(2)}) collective-permute-start(f32[1,128]{1,0:T(1,128)S(1)} %get-tuple-element.19), channel_id=1, source_target_pairs={{4,0},{8,4},{12,8},{5,1},{9,5},{13,9},{6,2},{10,6},{14,10},{7,3},{... | collective-permute-start | bytes 1544 | tf_op jit(solution)/shard_map/ppermute | solution.py:286
  16.5 1.6 %copy-start.2 = (bf16[1,1,4,1024,256]{4,3,2,1,0:T(8,128)(2,1)S(1)}, bf16[1,1,4,1024,256]{4,3,2,1,0:T(8,128)(2,1)}, u32[]{:S(2)}) copy-start(bf16[1,1,4,1024,256]{4,3,2,1,0:T(8,128)(2,1)} %param.12) | copy-start | bytes 6291460
  20.4 0.7 copy-start.9
  21.1 4.7 %collective-permute-start.8 = (f32[1024,256]{1,0:T(8,128)S(1)}, f32[1024,256]{1,0:T(8,128)}, u32[]{:S(2)}, u32[]{:S(2)}) collective-permute-start(f32[1024,256]{1,0:T(8,128)S(1)} %get-tuple-element.29), channel_id=1, source_target_pairs={{0,16},{16,0},{32,48},{48,32},{64,80},{80,64},{96,112},{112,96},{1... | collective-permute-start | bytes 3145736 | tf_op jit(solution)/shard_map/ppermute | solution.py:312
  23.0 1.0 copy-start.10
  27.2 68.0 %copy-start.5 = (f32[128,1024]{1,0:T(8,128)S(1)}, f32[128,1024]{1,0:T(8,128)}, u32[]{:S(2)}) copy-start(f32[128,1024]{1,0:T(8,128)} %elev_ref.3) | copy-start | bytes 1572868
  27.2 11.3 %collective-permute-start.9 = (f32[512,256]{1,0:T(8,128)S(1)}, f32[512,256]{1,0:T(8,128)}, u32[]{:S(2)}, u32[]{:S(2)}) collective-permute-start(f32[512,256]{1,0:T(8,128)S(1)} %constant_dynamic-slice_fusion.3), channel_id=1, source_target_pairs={{0,32},{16,496},{32,0},{48,80},{64,96},{80,48},{96,64},{112,144},{... | collective-permute-start | bytes 1572872 | tf_op jit(solution)/shard_map/ppermute | solution.py:321
  39.7 11.5 %collective-permute-start.10 = (f32[256,256]{1,0:T(8,128)S(1)}, f32[256,256]{1,0:T(8,128)S(1)}, u32[]{:S(2)}, u32[]{:S(2)}) collective-permute-start(f32[256,256]{1,0:T(8,128)S(1)} %constant_dynamic-slice_fusion.2), channel_id=1, source_target_pairs={{0,64},{16,464},{32,96},{48,496},{64,0},{80,144},{96,32},{112,176}... | collective-permute-start | bytes 786440 | tf_op jit(solution)/shard_map/ppermute | solution.py:321
  51.2 14.2 %collective-permute-start.11 = (f32[128,256]{1,0:T(8,128)S(1)}, f32[128,256]{1,0:T(8,128)S(1)}, u32[]{:S(2)}, u32[]{:S(2)}) collective-permute-start(f32[128,256]{1,0:T(8,128)S(1)} %constant_dynamic-slice_fusion.1), channel_id=1, source_target_pairs={{0,128},{16,400},{32,160},{48,432},{64,192},{80,464},{96,224},{112... | collective-permute-start | bytes 393224 | tf_op jit(solution)/shard_map/ppermute | solution.py:321
  65.4 31.1 %collective-permute-start.12 = (f32[64,256]{1,0:T(8,128)S(1)}, f32[64,256]{1,0:T(8,128)S(1)}, u32[]{:S(2)}, u32[]{:S(2)}) collective-permute-start(f32[64,256]{1,0:T(8,128)S(1)} %constant_dynamic-slice_fusion), channel_id=1, source_target_pairs={{0,256},{16,272},{32,288},{48,304},{64,320},{80,336},{96,352},{112... | collective-permute-start | bytes 196616 | tf_op jit(solution)/shard_map/ppermute | solution.py:321
  80.6 14.5 %collective-permute-start.4 = (f32[1,1024]{1,0:T(1,128)S(1)}, f32[1,1024]{1,0:T(1,128)S(1)}, u32[]{:S(2)}, u32[]{:S(2)}) collective-permute-start(f32[1,1024]{1,0:T(1,128)S(1)} %get-tuple-element.23), channel_id=1, source_target_pairs={{0,16},{16,32},{32,48},{48,64},{64,80},{80,96},{96,112},{112,128},... | collective-permute-start | bytes 12296 | tf_op jit(solution)/shard_map/ppermute | solution.py:285
  82.6 12.6 %collective-permute-start.5 = (f32[1,1024]{1,0:T(1,128)S(1)}, f32[1,1024]{1,0:T(1,128)S(1)}, u32[]{:S(2)}, u32[]{:S(2)}) collective-permute-start(f32[1,1024]{1,0:T(1,128)S(1)} %get-tuple-element.24), channel_id=1, source_target_pairs={{16,0},{32,16},{48,32},{64,48},{80,64},{96,80},{112,96},{128,112},... | collective-permute-start | bytes 12296 | tf_op jit(solution)/shard_map/ppermute | solution.py:286
  86.2 4.8 %collective-permute-start.6 = (f32[1,128]{1,0:T(1,128)S(1)}, f32[1,128]{1,0:T(1,128)S(1)}, u32[]{:S(2)}, u32[]{:S(2)}) collective-permute-start(f32[1,128]{1,0:T(1,128)S(1)} %get-tuple-element.25), channel_id=1, source_target_pairs={{0,4},{4,8},{8,12},{1,5},{5,9},{9,13},{2,6},{6,10},{10,14},{3,7},{... | collective-permute-start | bytes 1544 | tf_op jit(solution)/shard_map/ppermute | solution.py:285
  89.7 5.5 %collective-permute-start.7 = (f32[1,128]{1,0:T(1,128)S(1)}, f32[1,128]{1,0:T(1,128)S(1)}, u32[]{:S(2)}, u32[]{:S(2)}) collective-permute-start(f32[1,128]{1,0:T(1,128)S(1)} %get-tuple-element.26), channel_id=1, source_target_pairs={{4,0},{8,4},{12,8},{5,1},{9,5},{13,9},{6,2},{10,6},{14,10},{7,3},{... | collective-permute-start | bytes 1544 | tf_op jit(solution)/shard_map/ppermute | solution.py:286

commit v2 on v1

--- a/solution.py
+++ b/solution.py
@@ -1,5 +1,3 @@
-import functools
-
 import jax
 import jax.numpy as jnp
 from jax import lax
@@ -7,6 +5,7 @@
 from jax.experimental.pallas import tpu as pltpu
 from jax.sharding import PartitionSpec as P
 
+
 BS = 32
 DT = 0.2
 F32 = jnp.float32
@@ -21,6 +20,10 @@
 
 def vmem():
     return pl.BlockSpec(memory_space=pltpu.VMEM)
+
+
+def hbm():
+    return pl.BlockSpec(memory_space=pltpu.HBM)
 
 
 def params(limit=VLIM):
@@ -57,7 +60,12 @@
     )(a, a, a, a)
 
 
-def index_kernel(core_ref, patch_ref, owner_ref, idx_ref, dest_ref, sel_ref):
+def index_kernel(
+    place_ref, patch_ref, owner_ref, idx_ref, kap_ref, elev_ref, dest_ref, sel_ref, coef_ref
+):
+    for r in range(0, kap_ref.shape[0], 8):
+        e = elev_ref[r : r + 8, :]
+        coef_ref[r : r + 8, :] = DT * kap_ref[r : r + 8, :] / (1.0 + e * e)
     entries = patch_ref.shape[1]
     patches = owner_ref.shape[1]
     hot = lax.broadcasted_iota(I32, (patches, entries), 0) == patch_ref[...]
@@ -66,7 +74,7 @@
     row = lax.broadcasted_iota(I32, (16, patches), 0)
     parts = jnp.where(row == 0, owner >> 6, jnp.where(row == 1, owner & 63, 0))
     found = jnp.dot(parts.astype(F32).astype(BF16), hot, preferred_element_type=F32)
-    high = found[0:1, :].astype(I32) ^ core_ref[0]
+    high = found[0:1, :].astype(I32) ^ (place_ref[0] & 3)
     low = found[1:2, :].astype(I32)
     spot = jnp.zeros_like(high)
     for bit in range(5):
@@ -82,22 +90,23 @@
         )
 
 
-def indices(core, patch, owner, idx):
+def indices(place, patch, owner, idx, kappa, elev):
     entries = patch.shape[1]
     return pl.pallas_call(
         index_kernel,
-        in_specs=[pl.BlockSpec(memory_space=pltpu.SMEM), vmem(), vmem(), vmem()],
-        out_specs=[vmem(), vmem()],
+        in_specs=[pl.BlockSpec(memory_space=pltpu.SMEM)] + [vmem()] * 5,
+        out_specs=[vmem()] * 3,
         out_shape=[
             jax.ShapeDtypeStruct((1, entries), I32),
             jax.ShapeDtypeStruct((entries // 4, 4), I32),
+            whole(kappa.shape),
         ],
         compiler_params=params(),
         name="indices",
-    )(core, patch, owner, idx)
-
-
-def stencil(a_ref, kap_ref, elev_ref, n_ref, s_ref, wt, et, emit):
+    )(place, patch, owner, idx, kappa, elev)
+
+
+def stencil(a_ref, coef_of, n_ref, s_ref, wt, et, emit):
     rows, cols = a_ref.shape
     lane = lax.broadcasted_iota(I32, (8, cols), 1)
     sub = lax.broadcasted_iota(I32, (8, cols), 0)
@@ -114,10 +123,8 @@
             down = a_ref[r + 1 : r + 9, :]
         east = jnp.where(lane == cols - 1, et[r : r + 8, 0:1], pltpu.roll(x, cols - 1, 1))
         west = jnp.where(lane == 0, wt[r : r + 8, 0:1], pltpu.roll(x, 1, 1))
-        e = elev_ref[r : r + 8, :]
-        coef = DT * kap_ref[r : r + 8, :] / (1.0 + e * e)
         lap = down + up + east + west - 4.0 * x
-        emit(r, x, x + coef * lap)
+        emit(r, x, x + coef_of(r) * lap)
 
 
 def column(ref):
@@ -131,22 +138,26 @@
     return jnp.where(row == dest, 1.0, 0.0).astype(BF16)
 
 
-def gather_rows(out_ref, dest, hi, lo, first):
+def gather_rows(out_ref, dest, hi, lo, first, got_ref=None):
     rows = out_ref.shape[0]
     step = 256
     for k in range(rows // step):
         hot = hot_rows(dest, first + k * step, step)
         total = jnp.dot(hot, hi, preferred_element_type=F32)
         total += jnp.dot(hot, lo, preferred_element_type=F32)
+        if got_ref is not None:
+            total += got_ref[first + k * step : first + (k + 1) * step, :]
         out_ref[k * step : (k + 1) * step, :] = total
 
 
 def main_kernel(
-    a_ref, kap_ref, elev_ref, n_ref, s_ref, w_ref, e_ref, basis_ref, dest_ref, sel_ref,
+    a_ref, coef_ref, n_ref, s_ref, w_ref, e_ref, basis_ref, dest_ref, sel_ref,
     mid_ref, t_ref, b_ref, l_ref, r_ref, hi_ref, lo_ref, send_ref,
-    wt, et, g_ref, y_ref, c_ref,
+    wt, et, g_ref, y_ref, c_ref, table, sem,
 ):
     rows, cols = a_ref.shape
+    copy = pltpu.make_async_copy(basis_ref, table, sem)
+    copy.start()
     wt[...] = column(w_ref)
     et[...] = column(e_ref)
 
@@ -156,7 +167,7 @@
         for k in range(cols // 128):
             g_ref[k, r : r + 8, :] = g[:, k * 128 : (k + 1) * 128]
 
-    stencil(a_ref, kap_ref, elev_ref, n_ref, s_ref, wt, et, emit)
+    stencil(a_ref, lambda r: coef_ref[r : r + 8, :], n_ref, s_ref, wt, et, emit)
     nb = rows * cols // (BS * BS)
     chunk = lax.broadcasted_iota(I32, (8, 128), 1) // BS
     for br in range(rows // BS):
@@ -176,8 +187,9 @@
     lhs = jnp.concatenate(
         [y_ref[rh * nb : (rh + 1) * nb, :].astype(BF16) for rh in range(8)], axis=1
     )
+    copy.wait()
     products = [
-        jnp.dot(lhs, basis_ref[q], preferred_element_type=F32)
+        jnp.dot(lhs, table[q], preferred_element_type=F32)
         for q in range(basis_ref.shape[0])
     ]
     for o in range(4):
@@ -199,13 +211,13 @@
     r_ref[...] = mid_ref[:, cols - 128 : cols].T[127:128, :]
 
 
-def main(a, kappa, elev, halo, basis, dest, sel, total):
+def main(a, coef, halo, basis, dest, sel, total):
     rows, cols = a.shape
     entries = dest.shape[1]
     ncoef = basis.shape[-1]
     return pl.pallas_call(
         main_kernel,
-        in_specs=[vmem()] * 10,
+        in_specs=[vmem()] * 6 + [hbm()] + [vmem()] * 2,
         out_specs=[vmem()] * 8,
         out_shape=[
             whole((rows, cols)),
@@ -223,51 +235,77 @@
             pltpu.VMEM((cols // 128, rows, 128), F32),
             pltpu.VMEM((rows * cols // 128, 128), F32),
             pltpu.VMEM((2, entries, 128), F32),
+            pltpu.VMEM(basis.shape, BF16),
+            pltpu.SemaphoreType.DMA,
         ],
         compiler_params=params(),
         cost_estimate=pl.CostEstimate(
             flops=10**9, bytes_accessed=6 << 20, transcendentals=0
         ),
         name="main",
-    )(a, kappa, elev, *halo, basis, dest, sel)
-
-
-def keep_kernel(dest_ref, hi_ref, lo_ref, out_ref):
-    gather_rows(out_ref, dest_ref[...], hi_ref[...], lo_ref[...], 0)
-
-
-def keep_rows(dest, hi, lo, total):
+    )(a, coef, *halo, basis, dest, sel)
+
+
+def keep_kernel(dest_ref, hi_ref, lo_ref, got_ref, sent_ref, part_ref):
+    dest, hi, lo = dest_ref[...], hi_ref[...], lo_ref[...]
+    half = part_ref.shape[0]
+    gather_rows(sent_ref, dest, hi, lo, half, got_ref)
+    gather_rows(part_ref, dest, hi, lo, 0, got_ref)
+
+
+def keep_rows(dest, hi, lo, got):
+    half = whole((got.shape[0] // 2, got.shape[1]))
     return pl.pallas_call(
         keep_kernel,
-        in_specs=[vmem()] * 3,
-        out_specs=vmem(),
-        out_shape=whole((total // 2, hi.shape[1])),
+        in_specs=[vmem()] * 4,
+        out_specs=[vmem()] * 2,
+        out_shape=[half, half],
         compiler_params=params(),
         cost_estimate=pl.CostEstimate(
             flops=5 * 10**8, bytes_accessed=1 << 20, transcendentals=0
         ),
         name="keep",
-    )(dest, hi, lo)
-
-
-def last_kernel(a_ref, kap_ref, elev_ref, n_ref, s_ref, w_ref, e_ref, out_ref, wt, et):
+    )(dest, hi, lo, got)
+
+
+def last_kernel(
+    a_ref, kap_hbm, elev_hbm, n_ref, s_ref, w_ref, e_ref, out_ref, kap, elev, wt, et, sems
+):
+    copies = [
+        pltpu.make_async_copy(kap_hbm, kap, sems.at[0]),
+        pltpu.make_async_copy(elev_hbm, elev, sems.at[1]),
+    ]
+    for copy in copies:
+        copy.start()
     wt[...] = column(w_ref)
     et[...] = column(e_ref)
+    for copy in copies:
+        copy.wait()
 
     def emit(r, x, new):
         out_ref[r : r + 8, :] = new
 
-    stencil(a_ref, kap_ref, elev_ref, n_ref, s_ref, wt, et, emit)
+    def coef(r):
+        e = elev[r : r + 8, :]
+        return DT * kap[r : r + 8, :] / (1.0 + e * e)
+
+    stencil(a_ref, coef, n_ref, s_ref, wt, et, emit)
 
 
 def last(a, kappa, elev, halo):
     rows, cols = a.shape
     return pl.pallas_call(
         last_kernel,
-        in_specs=[vmem()] * 7,
+        in_specs=[vmem(), hbm(), hbm()] + [vmem()] * 4,
         out_specs=vmem(),
         out_shape=whole((rows, cols)),
-        scratch_shapes=[pltpu.VMEM((rows, 128), F32), pltpu.VMEM((rows, 128), F32)],
+        scratch_shapes=[
+            pltpu.VMEM((rows, cols), F32),
+            pltpu.VMEM((rows, cols), F32),
+            pltpu.VMEM((rows, 128), F32),
+            pltpu.VMEM((rows, 128), F32),
+            pltpu.SemaphoreType.DMA((2,)),
+        ],
         compiler_params=params(),
         cost_estimate=pl.CostEstimate(
             flops=10**7, bytes_accessed=2 << 20, transcendentals=0
@@ -276,15 +314,11 @@
     )(a, kappa, elev, *halo)
 
 
-def exchange(top, bottom, left, right):
-    halo = []
-    for axis, low, high in (("row", bottom, top), ("col", right, left)):
-        count = lax.axis_size(axis)
-        forward = [(i, i + 1) for i in range(count - 1)]
-        backward = [(target, source) for source, target in forward]
-        halo.append(lax.ppermute(low, axis, forward))
-        halo.append(lax.ppermute(high, axis, backward))
-    return halo
+def exchange(axis, low, high):
+    count = lax.axis_size(axis)
+    forward = [(i, i + 1) for i in range(count - 1)]
+    backward = [(target, source) for source, target in forward]
+    return [lax.ppermute(low, axis, forward), lax.ppermute(high, axis, backward)]
 
 
 def partners(n_chip, distance):
@@ -297,36 +331,42 @@
     return pairs
 
 
-def on_device(
+def compute(
     adj_final, kappa, elev_early, elev_late, basis, basis_index, intersection_patch, owner_row
 ):
     n_row = lax.axis_size("row")
     total = owner_row.shape[1]
     place = lax.axis_index("row").astype(I32)
-    core, chip = place & 1, place >> 1
-    halo = exchange(*edges(adj_final))
-    dest, sel = indices(core.reshape(1), intersection_patch[0], owner_row, basis_index[0])
+    chip = place >> 1
+    top, bottom, left, right = edges(adj_final)
+    halo = exchange("row", bottom, top) + exchange("col", right, left)
+    dest, sel, coef = indices(
+        place.reshape(1), intersection_patch[0], owner_row, basis_index[0], kappa, elev_late
+    )
     mid, top, bottom, left, right, hi, lo, send = main(
-        adj_final, kappa, elev_late, halo, basis[0, 0], dest, sel, total
+        adj_final, coef, halo, basis[0, 0], dest, sel, total
     )
     got = lax.ppermute(send, "row", [(i, i ^ 1) for i in range(n_row)])
-    part = keep_rows(dest, hi, lo, total) + got
-    halo = exchange(top, bottom, left, right)
-    adj_start = last(mid, kappa, elev_early, halo)
+    sent, part = keep_rows(dest, hi, lo, got)
+    halo_col = exchange("col", right, left)
+    halo_row = exchange("row", bottom, top)
+    adj_start = last(mid, kappa, elev_early, halo_row + halo_col)
     distance = 1
-    while distance < n_row // 2:
-        half = part.shape[0] // 2
+    while True:
+        got = lax.ppermute(sent, "row", partners(n_row // 2, distance))
+        total = part + got
+        distance *= 2
+        if distance == n_row // 2:
+            return (adj_start, total[None])
+        half = total.shape[0] // 2
         upper = (chip // distance) & 1
-        sent = lax.dynamic_slice_in_dim(part, (1 - upper) * half, half)
-        got = lax.ppermute(sent, "row", partners(n_row // 2, distance))
-        part = lax.dynamic_slice_in_dim(part, upper * half, half) + got
-        distance *= 2
-    return (adj_start, part[None])
+        sent = lax.dynamic_slice_in_dim(total, (1 - upper) * half, half)
+        part = lax.dynamic_slice_in_dim(total, upper * half, half)
 
 
 def solution(mesh):
     return jax.shard_map(
-        on_device,
+        compute,
         mesh=mesh,
         in_specs=(
             P(("mem", "row"), "col"),

time: 97.8 us -> 95.3 us (0.974)
  the two profiles are of different devices: /device:TPU:34 before, /device:TPU:38 now
where the time goes in v2:
time: 95.3 us; the launch traced here: 94.8 us
  starting transfers between devices  54.7 us (57%)
  waiting for transfers between devices  30.2 us (32%)
  Pallas kernels  5.39 us (6%)
  local copies, waits for them, and re-layouts  2.71 us (3%)
  between operations  0.99 us (1%)
    ppermute x4, starting transfers between devices, compute(): got = lax.ppermute(sent, 'row', partners(n_row // 2, distance))  32 us
    ppermute x4, waiting for transfers between devices, compute(): got = lax.ppermute(sent, 'row', partners(n_row // 2, distance))  20 us
    ppermute x4, starting transfers between devices, exchange(): lax.ppermute(low, axis, forward)  11 us
    ppermute x4, starting transfers between devices, exchange(): lax.ppermute(high, axis, backward)  9.87 us
    ppermute x4, waiting for transfers between devices, exchange(): lax.ppermute(high, axis, backward)  7.56 us
    unnamed x18, local copies, waits for them, and re-layouts  2.65 us
    ppermute x1, waiting for transfers between devices, compute(): got = lax.ppermute(send, 'row', [(i, i ^ 1) for i in range(n_row)])  2.63 us
    pallas_call x1, Pallas kernels, main(): pl.pallas_call(main_kernel, in_specs=[vmem()] * 6 + [hbm()] + [vmem()] *...  2.43 us
  transfers between devices with their start and end apart: 13, of which 6 were waited for; matrix products, arithmetic and copies ran while one was open for 0% of the time, Pallas kernels for 2%

profile of v2, /device:TPU:38, one launch (start us, length us, event | category | flops | bytes accessed | tf_op | source)
XLA Modules:
  0.0 94.8 jit_solution(16727098021893214587)
XLA Ops:
  0.6 1.0 %copy-done = f32[128,1024]{1,0:T(8,128)S(1)} copy-done((f32[128,1024]{1,0:T(8,128)S(1)}, f32[128,1024]{1,0:T(8,128)}, u32[]{:S(2)}) %copy-start) | copy-done | bytes 524312
  1.7 0.1 edges.1
  1.8 2.1 %collective-permute-start = (f32[1,1024]{1,0:T(1,128)S(1)}, f32[1,1024]{1,0:T(1,128)S(1)}, u32[]{:S(2)}, u32[]{:S(2)}) collective-permute-start(f32[1,1024]{1,0:T(1,128)S(1)} %get-tuple-element.20), channel_id=1, source_target_pairs={{0,16},{16,32},{32,48},{48,64},{64,80},{80,96},{96,112},{112,128},... | collective-permute-start | bytes 12296 | tf_op jit(solution)/shard_map/ppermute | solution.py:321
  3.9 3.6 %collective-permute-start.1 = (f32[1,1024]{1,0:T(1,128)S(1)}, f32[1,1024]{1,0:T(1,128)S(1)}, u32[]{:S(2)}, u32[]{:S(2)}) collective-permute-start(f32[1,1024]{1,0:T(1,128)S(1)} %get-tuple-element.21), channel_id=1, source_target_pairs={{16,0},{32,16},{48,32},{64,48},{80,64},{96,80},{112,96},{128,112},... | collective-permute-start | bytes 12296 | tf_op jit(solution)/shard_map/ppermute | solution.py:321
  7.5 3.5 %collective-permute-start.2 = (f32[1,128]{1,0:T(1,128)S(1)}, f32[1,128]{1,0:T(1,128)S(1)}, u32[]{:S(2)}, u32[]{:S(2)}) collective-permute-start(f32[1,128]{1,0:T(1,128)S(1)} %get-tuple-element.22), channel_id=1, source_target_pairs={{0,4},{4,8},{8,12},{1,5},{5,9},{9,13},{2,6},{6,10},{10,14},{3,7},{... | collective-permute-start | bytes 1544 | tf_op jit(solution)/shard_map/ppermute | solution.py:321
  11.0 1.3 %collective-permute-start.3 = (f32[1,128]{1,0:T(1,128)S(1)}, f32[1,128]{1,0:T(1,128)S(1)}, u32[]{:S(2)}, u32[]{:S(2)}) collective-permute-start(f32[1,128]{1,0:T(1,128)S(1)} %get-tuple-element.23), channel_id=1, source_target_pairs={{4,0},{8,4},{12,8},{5,1},{9,5},{13,9},{6,2},{10,6},{14,10},{7,3},{... | collective-permute-start | bytes 1544 | tf_op jit(solution)/shard_map/ppermute | solution.py:321
  12.4 0.7 indices.1
  13.0 0.0 collective-permute-done.2.w_ref
  13.1 3.4 %collective-permute-done.3.e_ref = f32[1,128]{1,0:T(1,128)S(1)} collective-permute-done((f32[1,128]{1,0:T(1,128)S(1)}, f32[1,128]{1,0:T(1,128)S(1)}, u32[]{:S(2)}, u32[]{:S(2)}) %collective-permute-start.3) | collective-permute-done | bytes 544 | tf_op jit(solution)/shard_map/ppermute | solution.py:321
  16.5 0.0 collective-permute-done.n_ref
  16.5 0.0 copy-start.8
  16.5 1.6 %copy-done.8 = bf16[1,1,4,1024,256]{4,3,2,1,0:T(8,128)(2,1)S(1)} copy-done((bf16[1,1,4,1024,256]{4,3,2,1,0:T(8,128)(2,1)S(1)}, bf16[1,1,4,1024,256]{4,3,2,1,0:T(8,128)(2,1)}, u32[]{:S(2)}) %copy-start.8) | copy-done | bytes 2097176
  18.1 2.4 %main.1 = (f32[128,1024]{1,0:T(8,128)S(1)}, f32[1,1024]{1,0:T(1,128)S(1)}, f32[1,1024]{1,0:T(1,128)S(1)}, f32[1,128]{1,0:T(1,128)S(1)}, f32[1,128]{1,0:T(1,128)S...) custom-call(f32[128,1024]{1,0:T(8,128)S(1)} %copy-done.1, ...), custom_call_target="tpu_custom_call" | custom-call | flops 1000000000 | bytes 6291456 | tf_op jit(solution)/shard_map/main/pallas_call | solution.py:218
  20.5 1.9 %collective-permute-start.8 = (f32[1024,256]{1,0:T(8,128)S(1)}, f32[1024,256]{1,0:T(8,128)S(1)}, u32[]{:S(2)}, u32[]{:S(2)}) collective-permute-start(f32[1024,256]{1,0:T(8,128)S(1)} %get-tuple-element.33), channel_id=1, source_target_pairs={{0,16},{16,0},{32,48},{48,32},{64,80},{80,64},{96,112},{112,96},{1... | collective-permute-start | bytes 3145736 | tf_op jit(solution)/shard_map/ppermute | solution.py:349
  22.4 2.6 %collective-permute-done.8.got_ref = f32[1024,256]{1,0:T(8,128)S(1)} collective-permute-done((f32[1024,256]{1,0:T(8,128)S(1)}, f32[1024,256]{1,0:T(8,128)S(1)}, u32[]{:S(2)}, u32[]{:S(2)}) %collective-permute-start.8) | collective-permute-done | bytes 1048608 | tf_op jit(solution)/shard_map/ppermute | solution.py:349
  25.1 0.7 keep.1
  25.8 0.0 copy-start.4
  25.8 2.1 %collective-permute-start.9 = (f32[512,256]{1,0:T(8,128)S(1)}, f32[512,256]{1,0:T(8,128)S(1)}, u32[]{:S(2)}, u32[]{:S(2)}) collective-permute-start(f32[512,256]{1,0:T(8,128)S(1)} %get-tuple-element.35), channel_id=1, source_target_pairs={{0,32},{16,496},{32,0},{48,80},{64,96},{80,48},{96,64},{112,144},{... | collective-permute-start | bytes 1572872 | tf_op jit(solution)/shard_map/ppermute | solution.py:356
  27.9 9.1 %collective-permute-done.9 = f32[512,256]{1,0:T(8,128)S(1)} collective-permute-done((f32[512,256]{1,0:T(8,128)S(1)}, f32[512,256]{1,0:T(8,128)S(1)}, u32[]{:S(2)}, u32[]{:S(2)}) %collective-permute-start.9) | collective-permute-done | bytes 524320 | tf_op jit(solution)/shard_map/ppermute | solution.py:356
  37.0 0.1 add.33
  37.1 5.2 %collective-permute-start.10 = (f32[256,256]{1,0:T(8,128)S(1)}, f32[256,256]{1,0:T(8,128)S(1)}, u32[]{:S(2)}, u32[]{:S(2)}) collective-permute-start(f32[256,256]{1,0:T(8,128)S(1)} %constant_dynamic-slice_fusion.2), channel_id=1, source_target_pairs={{0,64},{16,464},{32,96},{48,496},{64,0},{80,144},{96,32},{112,176}... | collective-permute-start | bytes 786440 | tf_op jit(solution)/shard_map/ppermute | solution.py:356
  42.3 6.2 %collective-permute-done.10 = f32[256,256]{1,0:T(8,128)S(1)} collective-permute-done((f32[256,256]{1,0:T(8,128)S(1)}, f32[256,256]{1,0:T(8,128)S(1)}, u32[]{:S(2)}, u32[]{:S(2)}) %collective-permute-start.10) | collective-permute-done | bytes 262176 | tf_op jit(solution)/shard_map/ppermute | solution.py:356
  48.6 9.5 %collective-permute-start.11 = (f32[128,256]{1,0:T(8,128)S(1)}, f32[128,256]{1,0:T(8,128)S(1)}, u32[]{:S(2)}, u32[]{:S(2)}) collective-permute-start(f32[128,256]{1,0:T(8,128)S(1)} %constant_dynamic-slice_fusion.1), channel_id=1, source_target_pairs={{0,128},{16,400},{32,160},{48,432},{64,192},{80,464},{96,224},{112... | collective-permute-start | bytes 393224 | tf_op jit(solution)/shard_map/ppermute | solution.py:356
  58.2 4.6 %collective-permute-done.11 = f32[128,256]{1,0:T(8,128)S(1)} collective-permute-done((f32[128,256]{1,0:T(8,128)S(1)}, f32[128,256]{1,0:T(8,128)S(1)}, u32[]{:S(2)}, u32[]{:S(2)}) %collective-permute-start.11) | collective-permute-done | bytes 131104 | tf_op jit(solution)/shard_map/ppermute | solution.py:356
  62.8 15.2 %collective-permute-start.12 = (f32[64,256]{1,0:T(8,128)S(1)}, f32[64,256]{1,0:T(8,128)S(1)}, u32[]{:S(2)}, u32[]{:S(2)}) collective-permute-start(f32[64,256]{1,0:T(8,128)S(1)} %constant_dynamic-slice_fusion), channel_id=1, source_target_pairs={{0,256},{16,272},{32,288},{48,304},{64,320},{80,336},{96,352},{112... | collective-permute-start | bytes 196616 | tf_op jit(solution)/shard_map/ppermute | solution.py:356
  78.1 1.9 %collective-permute-start.4 = (f32[1,1024]{1,0:T(1,128)S(1)}, f32[1,1024]{1,0:T(1,128)S(1)}, u32[]{:S(2)}, u32[]{:S(2)}) collective-permute-start(f32[1,1024]{1,0:T(1,128)S(1)} %get-tuple-element.27), channel_id=1, source_target_pairs={{0,16},{16,32},{32,48},{48,64},{64,80},{80,96},{96,112},{112,128},... | collective-permute-start | bytes 12296 | tf_op jit(solution)/shard_map/ppermute | solution.py:321
  80.0 3.6 %collective-permute-start.5 = (f32[1,1024]{1,0:T(1,128)S(1)}, f32[1,1024]{1,0:T(1,128)S(1)}, u32[]{:S(2)}, u32[]{:S(2)}) collective-permute-start(f32[1,1024]{1,0:T(1,128)S(1)} %get-tuple-element.28), channel_id=1, source_target_pairs={{16,0},{32,16},{48,32},{64,48},{80,64},{96,80},{112,96},{128,112},... | collective-permute-start | bytes 12296 | tf_op jit(solution)/shard_map/ppermute | solution.py:321
  83.6 3.5 %collective-permute-start.6 = (f32[1,128]{1,0:T(1,128)S(1)}, f32[1,128]{1,0:T(1,128)S(1)}, u32[]{:S(2)}, u32[]{:S(2)}) collective-permute-start(f32[1,128]{1,0:T(1,128)S(1)} %get-tuple-element.29), channel_id=1, source_target_pairs={{0,4},{4,8},{8,12},{1,5},{5,9},{9,13},{2,6},{6,10},{10,14},{3,7},{... | collective-permute-start | bytes 1544 | tf_op jit(solution)/shard_map/ppermute | solution.py:321
  87.1 1.3 %collective-permute-start.7 = (f32[1,128]{1,0:T(1,128)S(1)}, f32[1,128]{1,0:T(1,128)S(1)}, u32[]{:S(2)}, u32[]{:S(2)}) collective-permute-start(f32[1,128]{1,0:T(1,128)S(1)} %get-tuple-element.30), channel_id=1, source_target_pairs={{4,0},{8,4},{12,8},{5,1},{9,5},{13,9},{6,2},{10,6},{14,10},{7,3},{... | collective-permute-start | bytes 1544 | tf_op jit(solution)/shard_map/ppermute | solution.py:321
  88.5 4.1 %collective-permute-done.7.e_ref = f32[1,128]{1,0:T(1,128)S(1)} collective-permute-done((f32[1,128]{1,0:T(1,128)S(1)}, f32[1,128]{1,0:T(1,128)S(1)}, u32[]{:S(2)}, u32[]{:S(2)}) %collective-permute-start.7) | collective-permute-done | bytes 544 | tf_op jit(solution)/shard_map/ppermute | solution.py:321
  92.6 1.5 %last.1 = f32[128,1024]{1,0:T(8,128)} custom-call(f32[128,1024]{1,0:T(8,128)S(1)} %get-tuple-element.26.a_ref, f32[128,1024]{1,0:T(8,128)S(1)} %copy-done.2, f32[128,1024]{1,0:T(8,128)S(1)} %copy-done.4, f32[1,1024]{1,0:T(1,128)S(1)} %collective-permute-done.4.n_ref, f32[1,1024]{1,0:T(1,128)S(1)} %collective-permute-done.5.s_ref, ...), custom_call_target="tpu_custom_call" | custom-call | flops 10000000 | bytes 2097152 | tf_op jit(solution)/shard_map/last/pallas_call | solution.py:297
  94.1 0.6 add_bitcast_fusion
  (24 shorter events, 0.2 us)
Async XLA Ops:
  0.6 1.0 %copy-start = (f32[128,1024]{1,0:T(8,128)S(1)}, f32[128,1024]{1,0:T(8,128)}, u32[]{:S(2)}) copy-start(f32[128,1024]{1,0:T(8,128)} %a_ref.1) | copy-start | bytes 1572868
  1.7 10.6 %copy-start.2 = (f32[128,1024]{1,0:T(8,128)S(1)}, f32[128,1024]{1,0:T(8,128)}, u32[]{:S(2)}) copy-start(f32[128,1024]{1,0:T(8,128)} %kap_hbm.1) | copy-start | bytes 1572868
  1.7 10.6 %copy-start.3 = (f32[128,1024]{1,0:T(8,128)S(1)}, f32[128,1024]{1,0:T(8,128)}, u32[]{:S(2)}) copy-start(f32[128,1024]{1,0:T(8,128)} %elev_ref.1) | copy-start | bytes 1572868
  1.7 10.6 %copy-start.5 = (s32[1,2048]{1,0:T(1,128)S(1)}, s32[1,2048]{1,0:T(1,128)}, u32[]{:S(2)}) copy-start(s32[1,2048]{1,0:T(1,128)} %owner_ref.1) | copy-start | bytes 24580
  1.7 10.7 %copy-start.6 = (s32[1,1,512]{2,1,0:T(1,128)S(1)}, s32[1,1,512]{2,1,0:T(1,128)}, u32[]{:S(2)}) copy-start(s32[1,1,512]{2,1,0:T(1,128)} %param.14) | copy-start | bytes 6148
  1.7 10.7 %copy-start.7 = (s32[1,1,512]{2,1,0:T(1,128)S(1)}, s32[1,1,512]{2,1,0:T(1,128)}, u32[]{:S(2)}) copy-start(s32[1,1,512]{2,1,0:T(1,128)} %param.13) | copy-start | bytes 6148
  1.7 14.8 %copy-start.1 = (f32[128,1024]{1,0:T(8,128)S(1)}, f32[128,1024]{1,0:T(8,128)}, u32[]{:S(2)}) copy-start(f32[128,1024]{1,0:T(8,128)} %a_ref.1) | copy-start | bytes 1572868
  1.8 14.7 %collective-permute-start = (f32[1,1024]{1,0:T(1,128)S(1)}, f32[1,1024]{1,0:T(1,128)S(1)}, u32[]{:S(2)}, u32[]{:S(2)}) collective-permute-start(f32[1,1024]{1,0:T(1,128)S(1)} %get-tuple-element.20), channel_id=1, source_target_pairs={{0,16},{16,32},{32,48},{48,64},{64,80},{80,96},{96,112},{112,128},... | collective-permute-start | bytes 12296 | tf_op jit(solution)/shard_map/ppermute | solution.py:321
  3.9 12.6 %collective-permute-start.1 = (f32[1,1024]{1,0:T(1,128)S(1)}, f32[1,1024]{1,0:T(1,128)S(1)}, u32[]{:S(2)}, u32[]{:S(2)}) collective-permute-start(f32[1,1024]{1,0:T(1,128)S(1)} %get-tuple-element.21), channel_id=1, source_target_pairs={{16,0},{32,16},{48,32},{64,48},{80,64},{96,80},{112,96},{128,112},... | collective-permute-start | bytes 12296 | tf_op jit(solution)/shard_map/ppermute | solution.py:321
  7.5 5.5 %collective-permute-start.2 = (f32[1,128]{1,0:T(1,128)S(1)}, f32[1,128]{1,0:T(1,128)S(1)}, u32[]{:S(2)}, u32[]{:S(2)}) collective-permute-start(f32[1,128]{1,0:T(1,128)S(1)} %get-tuple-element.22), channel_id=1, source_target_pairs={{0,4},{4,8},{8,12},{1,5},{5,9},{9,13},{2,6},{6,10},{10,14},{3,7},{... | collective-permute-start | bytes 1544 | tf_op jit(solution)/shard_map/ppermute | solution.py:321
  11.0 5.5 %collective-permute-start.3 = (f32[1,128]{1,0:T(1,128)S(1)}, f32[1,128]{1,0:T(1,128)S(1)}, u32[]{:S(2)}, u32[]{:S(2)}) collective-permute-start(f32[1,128]{1,0:T(1,128)S(1)} %get-tuple-element.23), channel_id=1, source_target_pairs={{4,0},{8,4},{12,8},{5,1},{9,5},{13,9},{6,2},{10,6},{14,10},{7,3},{... | collective-permute-start | bytes 1544 | tf_op jit(solution)/shard_map/ppermute | solution.py:321
  16.5 1.6 %copy-start.8 = (bf16[1,1,4,1024,256]{4,3,2,1,0:T(8,128)(2,1)S(1)}, bf16[1,1,4,1024,256]{4,3,2,1,0:T(8,128)(2,1)}, u32[]{:S(2)}) copy-start(bf16[1,1,4,1024,256]{4,3,2,1,0:T(8,128)(2,1)} %param.12) | copy-start | bytes 6291460
  20.5 4.6 %collective-permute-start.8 = (f32[1024,256]{1,0:T(8,128)S(1)}, f32[1024,256]{1,0:T(8,128)S(1)}, u32[]{:S(2)}, u32[]{:S(2)}) collective-permute-start(f32[1024,256]{1,0:T(8,128)S(1)} %get-tuple-element.33), channel_id=1, source_target_pairs={{0,16},{16,0},{32,48},{48,32},{64,80},{80,64},{96,112},{112,96},{1... | collective-permute-start | bytes 3145736 | tf_op jit(solution)/shard_map/ppermute | solution.py:349
  25.8 66.8 %copy-start.4 = (f32[128,1024]{1,0:T(8,128)S(1)}, f32[128,1024]{1,0:T(8,128)}, u32[]{:S(2)}) copy-start(f32[128,1024]{1,0:T(8,128)} %elev_hbm.1) | copy-start | bytes 1572868
  25.8 11.2 %collective-permute-start.9 = (f32[512,256]{1,0:T(8,128)S(1)}, f32[512,256]{1,0:T(8,128)S(1)}, u32[]{:S(2)}, u32[]{:S(2)}) collective-permute-start(f32[512,256]{1,0:T(8,128)S(1)} %get-tuple-element.35), channel_id=1, source_target_pairs={{0,32},{16,496},{32,0},{48,80},{64,96},{80,48},{96,64},{112,144},{... | collective-permute-start | bytes 1572872 | tf_op jit(solution)/shard_map/ppermute | solution.py:356
  37.1 11.4 %collective-permute-start.10 = (f32[256,256]{1,0:T(8,128)S(1)}, f32[256,256]{1,0:T(8,128)S(1)}, u32[]{:S(2)}, u32[]{:S(2)}) collective-permute-start(f32[256,256]{1,0:T(8,128)S(1)} %constant_dynamic-slice_fusion.2), channel_id=1, source_target_pairs={{0,64},{16,464},{32,96},{48,496},{64,0},{80,144},{96,32},{112,176}... | collective-permute-start | bytes 786440 | tf_op jit(solution)/shard_map/ppermute | solution.py:356
  48.6 14.2 %collective-permute-start.11 = (f32[128,256]{1,0:T(8,128)S(1)}, f32[128,256]{1,0:T(8,128)S(1)}, u32[]{:S(2)}, u32[]{:S(2)}) collective-permute-start(f32[128,256]{1,0:T(8,128)S(1)} %constant_dynamic-slice_fusion.1), channel_id=1, source_target_pairs={{0,128},{16,400},{32,160},{48,432},{64,192},{80,464},{96,224},{112... | collective-permute-start | bytes 393224 | tf_op jit(solution)/shard_map/ppermute | solution.py:356
  62.8 31.3 %collective-permute-start.12 = (f32[64,256]{1,0:T(8,128)S(1)}, f32[64,256]{1,0:T(8,128)S(1)}, u32[]{:S(2)}, u32[]{:S(2)}) collective-permute-start(f32[64,256]{1,0:T(8,128)S(1)} %constant_dynamic-slice_fusion), channel_id=1, source_target_pairs={{0,256},{16,272},{32,288},{48,304},{64,320},{80,336},{96,352},{112... | collective-permute-start | bytes 196616 | tf_op jit(solution)/shard_map/ppermute | solution.py:356
  78.1 14.5 %collective-permute-start.4 = (f32[1,1024]{1,0:T(1,128)S(1)}, f32[1,1024]{1,0:T(1,128)S(1)}, u32[]{:S(2)}, u32[]{:S(2)}) collective-permute-start(f32[1,1024]{1,0:T(1,128)S(1)} %get-tuple-element.27), channel_id=1, source_target_pairs={{0,16},{16,32},{32,48},{48,64},{64,80},{80,96},{96,112},{112,128},... | collective-permute-start | bytes 12296 | tf_op jit(solution)/shard_map/ppermute | solution.py:321
  80.0 12.6 %collective-permute-start.5 = (f32[1,1024]{1,0:T(1,128)S(1)}, f32[1,1024]{1,0:T(1,128)S(1)}, u32[]{:S(2)}, u32[]{:S(2)}) collective-permute-start(f32[1,1024]{1,0:T(1,128)S(1)} %get-tuple-element.28), channel_id=1, source_target_pairs={{16,0},{32,16},{48,32},{64,48},{80,64},{96,80},{112,96},{128,112},... | collective-permute-start | bytes 12296 | tf_op jit(solution)/shard_map/ppermute | solution.py:321
  83.6 4.8 %collective-permute-start.6 = (f32[1,128]{1,0:T(1,128)S(1)}, f32[1,128]{1,0:T(1,128)S(1)}, u32[]{:S(2)}, u32[]{:S(2)}) collective-permute-start(f32[1,128]{1,0:T(1,128)S(1)} %get-tuple-element.29), channel_id=1, source_target_pairs={{0,4},{4,8},{8,12},{1,5},{5,9},{9,13},{2,6},{6,10},{10,14},{3,7},{... | collective-permute-start | bytes 1544 | tf_op jit(solution)/shard_map/ppermute | solution.py:321
  87.1 5.5 %collective-permute-start.7 = (f32[1,128]{1,0:T(1,128)S(1)}, f32[1,128]{1,0:T(1,128)S(1)}, u32[]{:S(2)}, u32[]{:S(2)}) collective-permute-start(f32[1,128]{1,0:T(1,128)S(1)} %get-tuple-element.30), channel_id=1, source_target_pairs={{4,0},{8,4},{12,8},{5,1},{9,5},{13,9},{6,2},{10,6},{14,10},{7,3},{... | collective-permute-start | bytes 1544 | tf_op jit(solution)/shard_map/ppermute | solution.py:321

commit v3 on v2

--- a/solution.py
+++ b/solution.py
@@ -1,3 +1,5 @@
+import functools
+
 import jax
 import jax.numpy as jnp
 from jax import lax
@@ -26,38 +28,67 @@
     return pl.BlockSpec(memory_space=pltpu.HBM)
 
 
+def in_hbm(x):
+    return pltpu.with_memory_space_constraint(x, pltpu.HBM)
+
+
 def params(limit=VLIM):
     return pltpu.CompilerParams(vmem_limit_bytes=limit)
 
 
-def edges_kernel(top_ref, bot_ref, left_ref, right_ref, t_ref, b_ref, l_ref, r_ref):
-    t_ref[...] = top_ref[0:1, :]
-    b_ref[...] = bot_ref[7:8, :]
+def edge_row(x, inner, kap, elev):
+    lane = lax.broadcasted_iota(I32, x.shape, 1)
+    last = x.shape[1] - 1
+    east = jnp.where(lane == last, 0.0, pltpu.roll(x, last, 1))
+    west = jnp.where(lane == 0, 0.0, pltpu.roll(x, 1, 1))
+    coef = DT * kap / (1.0 + elev * elev)
+    return x + coef * (inner + east + west - 4.0 * x), coef
+
+
+def edges_kernel(
+    top_ref, bot_ref, left_ref, right_ref, ktop_ref, kbot_ref, etop_ref, ebot_ref,
+    t_ref, b_ref, l_ref, r_ref,
+):
+    top, bot = top_ref[...], bot_ref[...]
+    partial, coef = edge_row(top, pltpu.roll(top, 7, 0), ktop_ref[...], etop_ref[...])
+    t_ref[0:1, :] = top[0:1, :]
+    t_ref[1:2, :] = partial[0:1, :]
+    t_ref[2:3, :] = coef[0:1, :]
+    partial, coef = edge_row(bot, pltpu.roll(bot, 1, 0), kbot_ref[...], ebot_ref[...])
+    b_ref[0:1, :] = bot[7:8, :]
+    b_ref[1:2, :] = partial[7:8, :]
+    b_ref[2:3, :] = coef[7:8, :]
     l_ref[...] = left_ref[...].T[0:1, :]
     r_ref[...] = right_ref[...].T[127:128, :]
 
 
-def edges(a):
+def edges(a, kappa, elev):
     rows, cols = a.shape
+    first = pl.BlockSpec((8, cols), lambda i: (0, 0))
+    final = pl.BlockSpec((8, cols), lambda i: (rows // 8 - 1, 0))
     return pl.pallas_call(
         edges_kernel,
         grid=(1,),
         in_specs=[
-            pl.BlockSpec((8, cols), lambda i: (0, 0)),
-            pl.BlockSpec((8, cols), lambda i: (rows // 8 - 1, 0)),
+            first,
+            final,
             pl.BlockSpec((rows, 128), lambda i: (0, 0)),
             pl.BlockSpec((rows, 128), lambda i: (0, cols // 128 - 1)),
+            first,
+            final,
+            first,
+            final,
         ],
         out_specs=[
-            pl.BlockSpec((1, cols), lambda i: (0, 0)),
-            pl.BlockSpec((1, cols), lambda i: (0, 0)),
+            pl.BlockSpec((3, cols), lambda i: (0, 0)),
+            pl.BlockSpec((3, cols), lambda i: (0, 0)),
             pl.BlockSpec((1, rows), lambda i: (0, 0)),
             pl.BlockSpec((1, rows), lambda i: (0, 0)),
         ],
-        out_shape=[whole((1, cols)), whole((1, cols)), whole((1, rows)), whole((1, rows))],
+        out_shape=[whole((3, cols)), whole((3, cols)), whole((1, rows)), whole((1, rows))],
         compiler_params=params(4 << 20),
         name="edges",
-    )(a, a, a, a)
+    )(a, a, a, a, kappa, kappa, elev, elev)
 
 
 def index_kernel(
@@ -106,7 +137,7 @@
     )(place, patch, owner, idx, kappa, elev)
 
 
-def stencil(a_ref, coef_of, n_ref, s_ref, wt, et, emit):
+def stencil(a_ref, coef_of, north, south, wt, et, emit):
     rows, cols = a_ref.shape
     lane = lax.broadcasted_iota(I32, (8, cols), 1)
     sub = lax.broadcasted_iota(I32, (8, cols), 0)
@@ -114,11 +145,11 @@
         r = 8 * i
         x = a_ref[r : r + 8, :]
         if i == 0:
-            up = jnp.where(sub == 0, n_ref[...], pltpu.roll(x, 1, 0))
+            up = jnp.where(sub == 0, north, pltpu.roll(x, 1, 0))
         else:
             up = a_ref[r - 1 : r + 7, :]
         if i == rows // 8 - 1:
-            down = jnp.where(sub == 7, s_ref[...], pltpu.roll(x, 7, 0))
+            down = jnp.where(sub == 7, south, pltpu.roll(x, 7, 0))
         else:
             down = a_ref[r + 1 : r + 9, :]
         east = jnp.where(lane == cols - 1, et[r : r + 8, 0:1], pltpu.roll(x, cols - 1, 1))
@@ -128,8 +159,7 @@
 
 
 def column(ref):
-    n = ref.shape[1]
-    return jnp.broadcast_to(ref[...], (128, n)).T
+    return jnp.broadcast_to(ref[:, 0:128], (128, 128)).T
 
 
 def hot_rows(dest, start, count):
@@ -152,11 +182,11 @@
 
 def main_kernel(
     a_ref, coef_ref, n_ref, s_ref, w_ref, e_ref, basis_ref, dest_ref, sel_ref,
-    mid_ref, t_ref, b_ref, l_ref, r_ref, hi_ref, lo_ref, send_ref,
-    wt, et, g_ref, y_ref, c_ref, table, sem,
+    mid_hbm, l_ref, r_ref, hi_ref, lo_ref, send_ref,
+    wt, et, g_ref, y_ref, c_ref, table, mid_ref, sems,
 ):
     rows, cols = a_ref.shape
-    copy = pltpu.make_async_copy(basis_ref, table, sem)
+    copy = pltpu.make_async_copy(basis_ref, table, sems.at[0])
     copy.start()
     wt[...] = column(w_ref)
     et[...] = column(e_ref)
@@ -167,7 +197,10 @@
         for k in range(cols // 128):
             g_ref[k, r : r + 8, :] = g[:, k * 128 : (k + 1) * 128]
 
-    stencil(a_ref, lambda r: coef_ref[r : r + 8, :], n_ref, s_ref, wt, et, emit)
+    north, south = n_ref[0:1, :], s_ref[0:1, :]
+    stencil(a_ref, lambda r: coef_ref[r : r + 8, :], north, south, wt, et, emit)
+    stored = pltpu.make_async_copy(mid_ref, mid_hbm, sems.at[1])
+    stored.start()
     nb = rows * cols // (BS * BS)
     chunk = lax.broadcasted_iota(I32, (8, 128), 1) // BS
     for br in range(rows // BS):
@@ -205,10 +238,13 @@
     hi_ref[...] = hi
     lo_ref[...] = lo
     gather_rows(send_ref, dest_ref[...], hi, lo, send_ref.shape[0])
-    t_ref[...] = mid_ref[0:1, :]
-    b_ref[...] = mid_ref[rows - 1 : rows, :]
-    l_ref[...] = mid_ref[:, 0:128].T[0:1, :]
-    r_ref[...] = mid_ref[:, cols - 128 : cols].T[127:128, :]
+    l_ref[:, 0:128] = mid_ref[:, 0:128].T[0:1, :]
+    r_ref[:, 0:128] = mid_ref[:, cols - 128 : cols].T[127:128, :]
+    lane = lax.broadcasted_iota(I32, (1, 128), 1)
+    for out, k in ((l_ref, 0), (r_ref, cols - 1)):
+        corner = jnp.where(lane == 1, south[:, k : k + 1], 0.0)
+        out[:, 128:256] = jnp.where(lane == 0, north[:, k : k + 1], corner)
+    stored.wait()
 
 
 def main(a, coef, halo, basis, dest, sel, total):
@@ -218,13 +254,11 @@
     return pl.pallas_call(
         main_kernel,
         in_specs=[vmem()] * 6 + [hbm()] + [vmem()] * 2,
-        out_specs=[vmem()] * 8,
+        out_specs=[hbm()] + [vmem()] * 5,
         out_shape=[
             whole((rows, cols)),
-            whole((1, cols)),
-            whole((1, cols)),
-            whole((1, rows)),
-            whole((1, rows)),
+            whole((1, 2 * rows)),
+            whole((1, 2 * rows)),
             jax.ShapeDtypeStruct((entries, ncoef), BF16),
             jax.ShapeDtypeStruct((entries, ncoef), BF16),
             whole((total // 2, ncoef)),
@@ -236,7 +270,8 @@
             pltpu.VMEM((rows * cols // 128, 128), F32),
             pltpu.VMEM((2, entries, 128), F32),
             pltpu.VMEM(basis.shape, BF16),
-            pltpu.SemaphoreType.DMA,
+            pltpu.VMEM((rows, cols), F32),
+            pltpu.SemaphoreType.DMA((2,)),
         ],
         compiler_params=params(),
         cost_estimate=pl.CostEstimate(
@@ -246,32 +281,31 @@
     )(a, coef, *halo, basis, dest, sel)
 
 
-def keep_kernel(dest_ref, hi_ref, lo_ref, got_ref, sent_ref, part_ref):
-    dest, hi, lo = dest_ref[...], hi_ref[...], lo_ref[...]
-    half = part_ref.shape[0]
-    gather_rows(sent_ref, dest, hi, lo, half, got_ref)
-    gather_rows(part_ref, dest, hi, lo, 0, got_ref)
-
-
-def keep_rows(dest, hi, lo, got):
-    half = whole((got.shape[0] // 2, got.shape[1]))
+def add_kernel(first, dest_ref, hi_ref, lo_ref, got_ref, out_ref):
+    gather_rows(out_ref, dest_ref[...], hi_ref[...], lo_ref[...], first, got_ref)
+
+
+def add_rows(first, count, dest, hi, lo, got):
+    ncoef = got.shape[1]
     return pl.pallas_call(
-        keep_kernel,
+        functools.partial(add_kernel, first),
         in_specs=[vmem()] * 4,
-        out_specs=[vmem()] * 2,
-        out_shape=[half, half],
+        out_specs=vmem(),
+        out_shape=whole((count, ncoef)),
         compiler_params=params(),
         cost_estimate=pl.CostEstimate(
-            flops=5 * 10**8, bytes_accessed=1 << 20, transcendentals=0
+            flops=3 * 10**8, bytes_accessed=1 << 20, transcendentals=0
         ),
-        name="keep",
+        name="add",
     )(dest, hi, lo, got)
 
 
 def last_kernel(
-    a_ref, kap_hbm, elev_hbm, n_ref, s_ref, w_ref, e_ref, out_ref, kap, elev, wt, et, sems
+    a_hbm, kap_hbm, elev_hbm, n_ref, s_ref, w_ref, e_ref, t_ref, b_ref, out_ref,
+    a_ref, kap, elev, wt, et, sems,
 ):
     copies = [
+        pltpu.make_async_copy(a_hbm, a_ref, sems.at[2]),
         pltpu.make_async_copy(kap_hbm, kap, sems.at[0]),
         pltpu.make_async_copy(elev_hbm, elev, sems.at[1]),
     ]
@@ -289,29 +323,37 @@
         e = elev[r : r + 8, :]
         return DT * kap[r : r + 8, :] / (1.0 + e * e)
 
-    stencil(a_ref, coef, n_ref, s_ref, wt, et, emit)
-
-
-def last(a, kappa, elev, halo):
+    lane = lax.broadcasted_iota(I32, (1, a_ref.shape[1]), 1)
+    beyond = []
+    for k, (ref, own) in enumerate(((n_ref, t_ref), (s_ref, b_ref))):
+        missing = own[0:1, :]
+        missing += jnp.where(lane == 0, w_ref[:, 128 + k : 129 + k], 0.0)
+        missing += jnp.where(lane == a_ref.shape[1] - 1, e_ref[:, 128 + k : 129 + k], 0.0)
+        beyond.append(ref[1:2, :] + ref[2:3, :] * missing)
+    stencil(a_ref, coef, *beyond, wt, et, emit)
+
+
+def last(a, kappa, elev, halo, own):
     rows, cols = a.shape
     return pl.pallas_call(
         last_kernel,
-        in_specs=[vmem(), hbm(), hbm()] + [vmem()] * 4,
+        in_specs=[hbm()] * 3 + [vmem()] * 6,
         out_specs=vmem(),
         out_shape=whole((rows, cols)),
         scratch_shapes=[
             pltpu.VMEM((rows, cols), F32),
             pltpu.VMEM((rows, cols), F32),
+            pltpu.VMEM((rows, cols), F32),
             pltpu.VMEM((rows, 128), F32),
             pltpu.VMEM((rows, 128), F32),
-            pltpu.SemaphoreType.DMA((2,)),
+            pltpu.SemaphoreType.DMA((3,)),
         ],
         compiler_params=params(),
         cost_estimate=pl.CostEstimate(
             flops=10**7, bytes_accessed=2 << 20, transcendentals=0
         ),
         name="last",
-    )(a, kappa, elev, *halo)
+    )(a, kappa, elev, *halo, *own)
 
 
 def exchange(axis, low, high):
@@ -338,19 +380,21 @@
     total = owner_row.shape[1]
     place = lax.axis_index("row").astype(I32)
     chip = place >> 1
-    top, bottom, left, right = edges(adj_final)
-    halo = exchange("row", bottom, top) + exchange("col", right, left)
+    top, bottom, left, right = edges(in_hbm(adj_final), in_hbm(kappa), in_hbm(elev_late))
+    halo_row = exchange("row", bottom, top)
+    halo = halo_row + exchange("col", right, left)
     dest, sel, coef = indices(
         place.reshape(1), intersection_patch[0], owner_row, basis_index[0], kappa, elev_late
     )
-    mid, top, bottom, left, right, hi, lo, send = main(
-        adj_final, coef, halo, basis[0, 0], dest, sel, total
+    mid, left, right, hi, lo, send = main(
+        adj_final, coef, halo, in_hbm(basis[0, 0]), dest, sel, total
     )
     got = lax.ppermute(send, "row", [(i, i ^ 1) for i in range(n_row)])
-    sent, part = keep_rows(dest, hi, lo, got)
+    half = got.shape[0] // 2
+    sent = add_rows(half, half, dest, hi, lo, got)
+    part = add_rows(0, half, dest, hi, lo, got)
     halo_col = exchange("col", right, left)
-    halo_row = exchange("row", bottom, top)
-    adj_start = last(mid, kappa, elev_early, halo_row + halo_col)
+    adj_start = last(mid, in_hbm(kappa), in_hbm(elev_early), halo_row + halo_col, (top, bottom))
     distance = 1
     while True:
         got = lax.ppermute(sent, "row", partners(n_row // 2, distance))

time: 95.3 us -> 90.5 us (0.950)
  the two profiles are of different devices: /device:TPU:38 before, /device:TPU:4 now
where the time goes in v3:
time: 90.5 us; the launch traced here: 90 us
  starting transfers between devices  49.1 us (54%)
  waiting for transfers between devices  30.9 us (34%)
  Pallas kernels  8.2 us (9%)
  between operations  0.98 us (1%)
    ppermute x4, starting transfers between devices, compute(): got = lax.ppermute(sent, 'row', partners(n_row // 2, distance))  33.2 us
    ppermute x4, waiting for transfers between devices, compute(): got = lax.ppermute(sent, 'row', partners(n_row // 2, distance))  21 us
    ppermute x3, starting transfers between devices, exchange(): lax.ppermute(low, axis, forward)  8.73 us
    ppermute x3, waiting for transfers between devices, exchange(): lax.ppermute(high, axis, backward)  7.56 us
    ppermute x3, starting transfers between devices, exchange(): lax.ppermute(high, axis, backward)  3.88 us
    ppermute x1, starting transfers between devices, compute(): got = lax.ppermute(send, 'row', [(i, i ^ 1) for i in range(n_row)])  3.31 us
    pallas_call x1, Pallas kernels, main(): pl.pallas_call(main_kernel, in_specs=[vmem()] * 6 + [hbm()] + [vmem()] *...  2.9 us
    pallas_call x1, Pallas kernels, last(): pl.pallas_call(last_kernel, in_specs=[hbm()] * 3 + [vmem()] * 6, out_spec...  2.57 us
  transfers between devices with their start and end apart: 11, of which 6 were waited for; matrix products, arithmetic and copies ran while one was open for 0% of the time, Pallas kernels for 4%

profile of v3, /device:TPU:4, one launch (start us, length us, event | category | flops | bytes accessed | tf_op | source)
XLA Modules:
  0.0 90.0 jit_solution(14178856522222621200)
XLA Ops:
  0.6 0.0 copy-start.1
  0.6 0.0 copy-start
  0.7 1.2 %edges.1 = (f32[3,1024]{1,0:T(4,128)S(1)}, f32[3,1024]{1,0:T(4,128)S(1)}, f32[1,128]{1,0:T(1,128)S(1)}, f32[1,128]{1,0:T(1,128)S(1)}) custom-call(f32[128,1024]{1,0:T(8,128)} %a_ref.1, f32[128,1024]{1,0:T(8,128)} %a_ref.1, f32[128,1024]{1,0:T(8,128)} %a_ref.1, f32[128,1024]{1,0:T(8,128)} %a_ref.1, f32[128,1024]{1,0:T(8,128)} %kap_hbm.1, ...), custom_call_target="tpu_custom_call" | custom-call | tf_op jit(solution)/shard_map/edges/pallas_call | solution.py:69
  1.9 1.7 %collective-permute-start = (f32[3,1024]{1,0:T(4,128)S(1)}, f32[3,1024]{1,0:T(4,128)S(1)}, u32[]{:S(2)}, u32[]{:S(2)}) collective-permute-start(f32[3,1024]{1,0:T(4,128)S(1)} %get-tuple-element.16.b_ref), channel_id=1, source_target_pairs={{0,16},{16,32},{32,48},{48,64},{64,80},{80,96},{96,112},{112,128},... | collective-permute-start | bytes 36872 | tf_op jit(solution)/shard_map/ppermute | solution.py:363
  3.6 1.3 %collective-permute-start.1 = (f32[3,1024]{1,0:T(4,128)S(1)}, f32[3,1024]{1,0:T(4,128)S(1)}, u32[]{:S(2)}, u32[]{:S(2)}) collective-permute-start(f32[3,1024]{1,0:T(4,128)S(1)} %get-tuple-element.17.t_ref), channel_id=1, source_target_pairs={{16,0},{32,16},{48,32},{64,48},{80,64},{96,80},{112,96},{128,112},... | collective-permute-start | bytes 36872 | tf_op jit(solution)/shard_map/ppermute | solution.py:363
  4.9 3.5 %collective-permute-start.2 = (f32[1,128]{1,0:T(1,128)S(1)}, f32[1,128]{1,0:T(1,128)S(1)}, u32[]{:S(2)}, u32[]{:S(2)}) collective-permute-start(f32[1,128]{1,0:T(1,128)S(1)} %get-tuple-element.18), channel_id=1, source_target_pairs={{0,4},{4,8},{8,12},{1,5},{5,9},{9,13},{2,6},{6,10},{10,14},{3,7},{... | collective-permute-start | bytes 1544 | tf_op jit(solution)/shard_map/ppermute | solution.py:363
  8.4 1.3 %collective-permute-start.3 = (f32[1,128]{1,0:T(1,128)S(1)}, f32[1,128]{1,0:T(1,128)S(1)}, u32[]{:S(2)}, u32[]{:S(2)}) collective-permute-start(f32[1,128]{1,0:T(1,128)S(1)} %get-tuple-element.19), channel_id=1, source_target_pairs={{4,0},{8,4},{12,8},{5,1},{9,5},{13,9},{6,2},{10,6},{14,10},{7,3},{... | collective-permute-start | bytes 1544 | tf_op jit(solution)/shard_map/ppermute | solution.py:363
  9.8 0.7 indices.1
  10.5 0.0 collective-permute-done.2.w_ref
  10.5 3.4 %collective-permute-done.3.e_ref = f32[1,128]{1,0:T(1,128)S(1)} collective-permute-done((f32[1,128]{1,0:T(1,128)S(1)}, f32[1,128]{1,0:T(1,128)S(1)}, u32[]{:S(2)}, u32[]{:S(2)}) %collective-permute-start.3) | collective-permute-done | bytes 544 | tf_op jit(solution)/shard_map/ppermute | solution.py:363
  13.9 0.0 collective-permute-done.n_ref
  13.9 0.0 collective-permute-done.1.s_ref
  13.9 2.9 %main.1 = (f32[128,1024]{1,0:T(8,128)S(1)}, f32[1,256]{1,0:T(1,128)S(1)}, f32[1,256]{1,0:T(1,128)S(1)}, bf16[512,256]{1,0:T(8,128)(2,1)S(1)}, bf16[512,256]{1,0:T(8,128)(2,1)S(1)}, /*index=5*/f32[1024,256]{1,0:T(8,128)S(1)}) custom-call(f32[128,1024]{1,0:T(8,128)S(1)} %copy-done.1, f32[128,1024]{1,0:T(8,128)S(1)} %get-tuple-element.15.coef_ref, ...), custom_call_target="tpu_custom_call" | custom-call | flops 1000000000 | bytes 6291456 | tf_op jit(solution)/shard_map/main/pallas_call | solution.py:254
  16.8 3.3 %collective-permute-start.6 = (f32[1024,256]{1,0:T(8,128)S(1)}, f32[1024,256]{1,0:T(8,128)S(1)}, u32[]{:S(2)}, u32[]{:S(2)}) collective-permute-start(f32[1024,256]{1,0:T(8,128)S(1)} %get-tuple-element.27), channel_id=1, source_target_pairs={{0,16},{16,0},{32,48},{48,32},{64,80},{80,64},{96,112},{112,96},{1... | collective-permute-start | bytes 3145736 | tf_op jit(solution)/shard_map/ppermute | solution.py:392
  20.1 2.3 %collective-permute-done.6.got_ref = f32[1024,256]{1,0:T(8,128)S(1)} collective-permute-done((f32[1024,256]{1,0:T(8,128)S(1)}, f32[1024,256]{1,0:T(8,128)S(1)}, u32[]{:S(2)}, u32[]{:S(2)}) %collective-permute-start.6) | collective-permute-done | bytes 1048608 | tf_op jit(solution)/shard_map/ppermute | solution.py:392
  22.4 0.4 add.49
  22.8 5.3 %collective-permute-start.7 = (f32[512,256]{1,0:T(8,128)S(1)}, f32[512,256]{1,0:T(8,128)S(1)}, u32[]{:S(2)}, u32[]{:S(2)}) collective-permute-start(f32[512,256]{1,0:T(8,128)S(1)} %add.49), channel_id=1, source_target_pairs={{0,32},{16,496},{32,0},{48,80},{64,96},{80,48},{96,64},{112,144},{... | collective-permute-start | bytes 1572872 | tf_op jit(solution)/shard_map/ppermute | solution.py:400
  28.2 0.4 add.48
  28.6 6.7 %collective-permute-done.7 = f32[512,256]{1,0:T(8,128)S(1)} collective-permute-done((f32[512,256]{1,0:T(8,128)S(1)}, f32[512,256]{1,0:T(8,128)S(1)}, u32[]{:S(2)}, u32[]{:S(2)}) %collective-permute-start.7) | collective-permute-done | bytes 524320 | tf_op jit(solution)/shard_map/ppermute | solution.py:400
  35.3 0.1 add.35
  35.4 5.3 %collective-permute-start.8 = (f32[256,256]{1,0:T(8,128)S(1)}, f32[256,256]{1,0:T(8,128)S(1)}, u32[]{:S(2)}, u32[]{:S(2)}) collective-permute-start(f32[256,256]{1,0:T(8,128)S(1)} %constant_dynamic-slice_fusion.2), channel_id=1, source_target_pairs={{0,64},{16,464},{32,96},{48,496},{64,0},{80,144},{96,32},{112,176}... | collective-permute-start | bytes 786440 | tf_op jit(solution)/shard_map/ppermute | solution.py:400
  40.7 7.1 %collective-permute-done.8 = f32[256,256]{1,0:T(8,128)S(1)} collective-permute-done((f32[256,256]{1,0:T(8,128)S(1)}, f32[256,256]{1,0:T(8,128)S(1)}, u32[]{:S(2)}, u32[]{:S(2)}) %collective-permute-start.8) | collective-permute-done | bytes 262176 | tf_op jit(solution)/shard_map/ppermute | solution.py:400
  47.9 10.0 %collective-permute-start.9 = (f32[128,256]{1,0:T(8,128)S(1)}, f32[128,256]{1,0:T(8,128)S(1)}, u32[]{:S(2)}, u32[]{:S(2)}) collective-permute-start(f32[128,256]{1,0:T(8,128)S(1)} %constant_dynamic-slice_fusion.1), channel_id=1, source_target_pairs={{0,128},{16,400},{32,160},{48,432},{64,192},{80,464},{96,224},{112... | collective-permute-start | bytes 393224 | tf_op jit(solution)/shard_map/ppermute | solution.py:400
  57.9 7.2 %collective-permute-done.9 = f32[128,256]{1,0:T(8,128)S(1)} collective-permute-done((f32[128,256]{1,0:T(8,128)S(1)}, f32[128,256]{1,0:T(8,128)S(1)}, u32[]{:S(2)}, u32[]{:S(2)}) %collective-permute-start.9) | collective-permute-done | bytes 131104 | tf_op jit(solution)/shard_map/ppermute | solution.py:400
  65.2 12.7 %collective-permute-start.10 = (f32[64,256]{1,0:T(8,128)S(1)}, f32[64,256]{1,0:T(8,128)S(1)}, u32[]{:S(2)}, u32[]{:S(2)}) collective-permute-start(f32[64,256]{1,0:T(8,128)S(1)} %constant_dynamic-slice_fusion), channel_id=1, source_target_pairs={{0,256},{16,272},{32,288},{48,304},{64,320},{80,336},{96,352},{112... | collective-permute-start | bytes 196616 | tf_op jit(solution)/shard_map/ppermute | solution.py:400
  77.8 3.5 %collective-permute-start.4 = (f32[1,256]{1,0:T(1,128)S(1)}, f32[1,256]{1,0:T(1,128)S(1)}, u32[]{:S(2)}, u32[]{:S(2)}) collective-permute-start(f32[1,256]{1,0:T(1,128)S(1)} %get-tuple-element.23), channel_id=1, source_target_pairs={{0,4},{4,8},{8,12},{1,5},{5,9},{9,13},{2,6},{6,10},{10,14},{3,7},{... | collective-permute-start | bytes 3080 | tf_op jit(solution)/shard_map/ppermute | solution.py:363
  81.3 1.3 %collective-permute-start.5 = (f32[1,256]{1,0:T(1,128)S(1)}, f32[1,256]{1,0:T(1,128)S(1)}, u32[]{:S(2)}, u32[]{:S(2)}) collective-permute-start(f32[1,256]{1,0:T(1,128)S(1)} %get-tuple-element.24), channel_id=1, source_target_pairs={{4,0},{8,4},{12,8},{5,1},{9,5},{13,9},{6,2},{10,6},{14,10},{7,3},{... | collective-permute-start | bytes 3080 | tf_op jit(solution)/shard_map/ppermute | solution.py:363
  82.6 0.0 collective-permute-done.4.w_ref
  82.7 4.2 %collective-permute-done.5.e_ref = f32[1,256]{1,0:T(1,128)S(1)} collective-permute-done((f32[1,256]{1,0:T(1,128)S(1)}, f32[1,256]{1,0:T(1,128)S(1)}, u32[]{:S(2)}, u32[]{:S(2)}) %collective-permute-start.5) | collective-permute-done | bytes 1056 | tf_op jit(solution)/shard_map/ppermute | solution.py:363
  86.8 2.6 %last.1 = f32[128,1024]{1,0:T(8,128)} custom-call(f32[128,1024]{1,0:T(8,128)S(1)} %get-tuple-element.22.a_hbm, f32[128,1024]{1,0:T(8,128)} %kap_hbm.1, f32[128,1024]{1,0:T(8,128)} %elev_hbm.1, f32[3,1024]{1,0:T(4,128)S(1)} %collective-permute-done.n_ref, f32[3,1024]{1,0:T(4,128)S(1)} %collective-permute-done.1.s_ref, ...), custom_call_target="tpu_custom_call" | custom-call | flops 10000000 | bytes 2097152 | tf_op jit(solution)/shard_map/last/pallas_call | solution.py:338
  89.4 0.0 collective-permute-done.10
  89.4 0.6 add_bitcast_fusion
  (15 shorter events, 0.1 us)
Async XLA Ops:
  0.6 13.2 %copy-start.1 = (f32[128,1024]{1,0:T(8,128)S(1)}, f32[128,1024]{1,0:T(8,128)}, u32[]{:S(2)}) copy-start(f32[128,1024]{1,0:T(8,128)} %a_ref.1) | copy-start | bytes 1572868
  0.6 9.1 %copy-start = (f32[128,1024]{1,0:T(8,128)S(1)}, f32[128,1024]{1,0:T(8,128)}, u32[]{:S(2)}) copy-start(f32[128,1024]{1,0:T(8,128)} %kap_hbm.1) | copy-start | bytes 1572868
  0.7 9.1 %copy-start.2 = (f32[128,1024]{1,0:T(8,128)S(1)}, f32[128,1024]{1,0:T(8,128)}, u32[]{:S(2)}) copy-start(f32[128,1024]{1,0:T(8,128)} %ebot_ref.1) | copy-start | bytes 1572868
  0.7 9.1 %copy-start.4 = (s32[1,1,512]{2,1,0:T(1,128)S(1)}, s32[1,1,512]{2,1,0:T(1,128)}, u32[]{:S(2)}) copy-start(s32[1,1,512]{2,1,0:T(1,128)} %param.14) | copy-start | bytes 6148
  0.7 9.1 %copy-start.3 = (s32[1,2048]{1,0:T(1,128)S(1)}, s32[1,2048]{1,0:T(1,128)}, u32[]{:S(2)}) copy-start(s32[1,2048]{1,0:T(1,128)} %owner_ref.1) | copy-start | bytes 24580
  0.7 9.1 %copy-start.5 = (s32[1,1,512]{2,1,0:T(1,128)S(1)}, s32[1,1,512]{2,1,0:T(1,128)}, u32[]{:S(2)}) copy-start(s32[1,1,512]{2,1,0:T(1,128)} %param.13) | copy-start | bytes 6148
  1.9 12.0 %collective-permute-start = (f32[3,1024]{1,0:T(4,128)S(1)}, f32[3,1024]{1,0:T(4,128)S(1)}, u32[]{:S(2)}, u32[]{:S(2)}) collective-permute-start(f32[3,1024]{1,0:T(4,128)S(1)} %get-tuple-element.16.b_ref), channel_id=1, source_target_pairs={{0,16},{16,32},{32,48},{48,64},{64,80},{80,96},{96,112},{112,128},... | collective-permute-start | bytes 36872 | tf_op jit(solution)/shard_map/ppermute | solution.py:363
  3.6 10.3 %collective-permute-start.1 = (f32[3,1024]{1,0:T(4,128)S(1)}, f32[3,1024]{1,0:T(4,128)S(1)}, u32[]{:S(2)}, u32[]{:S(2)}) collective-permute-start(f32[3,1024]{1,0:T(4,128)S(1)} %get-tuple-element.17.t_ref), channel_id=1, source_target_pairs={{16,0},{32,16},{48,32},{64,48},{80,64},{96,80},{112,96},{128,112},... | collective-permute-start | bytes 36872 | tf_op jit(solution)/shard_map/ppermute | solution.py:363
  4.9 5.5 %collective-permute-start.2 = (f32[1,128]{1,0:T(1,128)S(1)}, f32[1,128]{1,0:T(1,128)S(1)}, u32[]{:S(2)}, u32[]{:S(2)}) collective-permute-start(f32[1,128]{1,0:T(1,128)S(1)} %get-tuple-element.18), channel_id=1, source_target_pairs={{0,4},{4,8},{8,12},{1,5},{5,9},{9,13},{2,6},{6,10},{10,14},{3,7},{... | collective-permute-start | bytes 1544 | tf_op jit(solution)/shard_map/ppermute | solution.py:363
  8.4 5.5 %collective-permute-start.3 = (f32[1,128]{1,0:T(1,128)S(1)}, f32[1,128]{1,0:T(1,128)S(1)}, u32[]{:S(2)}, u32[]{:S(2)}) collective-permute-start(f32[1,128]{1,0:T(1,128)S(1)} %get-tuple-element.19), channel_id=1, source_target_pairs={{4,0},{8,4},{12,8},{5,1},{9,5},{13,9},{6,2},{10,6},{14,10},{7,3},{... | collective-permute-start | bytes 1544 | tf_op jit(solution)/shard_map/ppermute | solution.py:363
  16.8 5.6 %collective-permute-start.6 = (f32[1024,256]{1,0:T(8,128)S(1)}, f32[1024,256]{1,0:T(8,128)S(1)}, u32[]{:S(2)}, u32[]{:S(2)}) collective-permute-start(f32[1024,256]{1,0:T(8,128)S(1)} %get-tuple-element.27), channel_id=1, source_target_pairs={{0,16},{16,0},{32,48},{48,32},{64,80},{80,64},{96,112},{112,96},{1... | collective-permute-start | bytes 3145736 | tf_op jit(solution)/shard_map/ppermute | solution.py:392
  22.8 12.5 %collective-permute-start.7 = (f32[512,256]{1,0:T(8,128)S(1)}, f32[512,256]{1,0:T(8,128)S(1)}, u32[]{:S(2)}, u32[]{:S(2)}) collective-permute-start(f32[512,256]{1,0:T(8,128)S(1)} %add.49), channel_id=1, source_target_pairs={{0,32},{16,496},{32,0},{48,80},{64,96},{80,48},{96,64},{112,144},{... | collective-permute-start | bytes 1572872 | tf_op jit(solution)/shard_map/ppermute | solution.py:400
  35.4 12.4 %collective-permute-start.8 = (f32[256,256]{1,0:T(8,128)S(1)}, f32[256,256]{1,0:T(8,128)S(1)}, u32[]{:S(2)}, u32[]{:S(2)}) collective-permute-start(f32[256,256]{1,0:T(8,128)S(1)} %constant_dynamic-slice_fusion.2), channel_id=1, source_target_pairs={{0,64},{16,464},{32,96},{48,496},{64,0},{80,144},{96,32},{112,176}... | collective-permute-start | bytes 786440 | tf_op jit(solution)/shard_map/ppermute | solution.py:400
  47.9 17.2 %collective-permute-start.9 = (f32[128,256]{1,0:T(8,128)S(1)}, f32[128,256]{1,0:T(8,128)S(1)}, u32[]{:S(2)}, u32[]{:S(2)}) collective-permute-start(f32[128,256]{1,0:T(8,128)S(1)} %constant_dynamic-slice_fusion.1), channel_id=1, source_target_pairs={{0,128},{16,400},{32,160},{48,432},{64,192},{80,464},{96,224},{112... | collective-permute-start | bytes 393224 | tf_op jit(solution)/shard_map/ppermute | solution.py:400
  65.2 24.2 %collective-permute-start.10 = (f32[64,256]{1,0:T(8,128)S(1)}, f32[64,256]{1,0:T(8,128)S(1)}, u32[]{:S(2)}, u32[]{:S(2)}) collective-permute-start(f32[64,256]{1,0:T(8,128)S(1)} %constant_dynamic-slice_fusion), channel_id=1, source_target_pairs={{0,256},{16,272},{32,288},{48,304},{64,320},{80,336},{96,352},{112... | collective-permute-start | bytes 196616 | tf_op jit(solution)/shard_map/ppermute | solution.py:400
  77.8 4.8 %collective-permute-start.4 = (f32[1,256]{1,0:T(1,128)S(1)}, f32[1,256]{1,0:T(1,128)S(1)}, u32[]{:S(2)}, u32[]{:S(2)}) collective-permute-start(f32[1,256]{1,0:T(1,128)S(1)} %get-tuple-element.23), channel_id=1, source_target_pairs={{0,4},{4,8},{8,12},{1,5},{5,9},{9,13},{2,6},{6,10},{10,14},{3,7},{... | collective-permute-start | bytes 3080 | tf_op jit(solution)/shard_map/ppermute | solution.py:363
  81.3 5.5 %collective-permute-start.5 = (f32[1,256]{1,0:T(1,128)S(1)}, f32[1,256]{1,0:T(1,128)S(1)}, u32[]{:S(2)}, u32[]{:S(2)}) collective-permute-start(f32[1,256]{1,0:T(1,128)S(1)} %get-tuple-element.24), channel_id=1, source_target_pairs={{4,0},{8,4},{12,8},{5,1},{9,5},{13,9},{6,2},{10,6},{14,10},{7,3},{... | collective-permute-start | bytes 3080 | tf_op jit(solution)/shard_map/ppermute | solution.py:363

commit v4 on v3

--- a/solution.py
+++ b/solution.py
@@ -34,6 +34,18 @@
 
 def params(limit=VLIM):
     return pltpu.CompilerParams(vmem_limit_bytes=limit)
+
+
+def paths(n_chip):
+    steps = n_chip.bit_length() - 1
+    spots = [0] * n_chip
+    for path in range(n_chip):
+        at = 0
+        for step in range(steps):
+            if (path >> (steps - 1 - step)) & 1:
+                at += -swing(step) if at % 2 else swing(step)
+        spots[at % n_chip] = path
+    return spots
 
 
 def edge_row(x, inner, kap, elev):
@@ -105,11 +117,16 @@
     row = lax.broadcasted_iota(I32, (16, patches), 0)
     parts = jnp.where(row == 0, owner >> 6, jnp.where(row == 1, owner & 63, 0))
     found = jnp.dot(parts.astype(F32).astype(BF16), hot, preferred_element_type=F32)
-    high = found[0:1, :].astype(I32) ^ (place_ref[0] & 3)
+    high = found[0:1, :].astype(I32)
+    core, chip = place_ref[0] & 1, place_ref[0] >> 1
+    n_chip = patches // 128
+    mirror = (chip + high) & 1
+    away = (high >> 1) - chip
+    away = jnp.where(mirror == 1, -away, away) & (n_chip - 1)
     low = found[1:2, :].astype(I32)
-    spot = jnp.zeros_like(high)
-    for bit in range(5):
-        spot = spot | (((high >> bit) & 1) << (4 - bit))
+    spot = ((high & 1) ^ core) * n_chip
+    for d, path in enumerate(paths(n_chip)):
+        spot += jnp.where(away == d, path, 0)
     dest_ref[...] = spot * 64 + low
     nb = entries // 4
     lane = lax.broadcasted_iota(I32, (nb, entries), 1)
@@ -363,12 +380,16 @@
     return [lax.ppermute(low, axis, forward), lax.ppermute(high, axis, backward)]
 
 
-def partners(n_chip, distance):
+def swing(step):
+    return (1 - (-2) ** (step + 1)) // 3
+
+
+def partners(n_chip, step):
     pairs = []
     for z in range(n_chip):
         for core in range(2):
-            low = (z // distance) % 2 == core
-            other = (z + (distance if low else -distance)) % n_chip
+            sign = -1 if (z + core) % 2 else 1
+            other = (z + sign * swing(step)) % n_chip
             pairs.append((2 * z + core, 2 * other + core))
     return pairs
 
@@ -379,7 +400,6 @@
     n_row = lax.axis_size("row")
     total = owner_row.shape[1]
     place = lax.axis_index("row").astype(I32)
-    chip = place >> 1
     top, bottom, left, right = edges(in_hbm(adj_final), in_hbm(kappa), in_hbm(elev_late))
     halo_row = exchange("row", bottom, top)
     halo = halo_row + exchange("col", right, left)
@@ -395,17 +415,14 @@
     part = add_rows(0, half, dest, hi, lo, got)
     halo_col = exchange("col", right, left)
     adj_start = last(mid, in_hbm(kappa), in_hbm(elev_early), halo_row + halo_col, (top, bottom))
-    distance = 1
-    while True:
-        got = lax.ppermute(sent, "row", partners(n_row // 2, distance))
-        total = part + got
-        distance *= 2
-        if distance == n_row // 2:
-            return (adj_start, total[None])
-        half = total.shape[0] // 2
-        upper = (chip // distance) & 1
-        sent = lax.dynamic_slice_in_dim(total, (1 - upper) * half, half)
-        part = lax.dynamic_slice_in_dim(total, upper * half, half)
+    steps = (n_row // 2).bit_length() - 1
+    for step in range(steps):
+        got = lax.ppermute(sent, "row", partners(n_row // 2, step))
+        if step == steps - 1:
+            return (adj_start, (part + got)[None])
+        half = part.shape[0] // 2
+        sent = part[half:] + got[half:]
+        part = part[:half] + got[:half]
 
 
 def solution(mesh):

time: 90.5 us -> 81.8 us (0.904)
  starting transfers between devices: 49.1 us -> 42.4 us
  waiting for transfers between devices: 30.9 us -> 29.1 us
    ppermute x4, starting transfers between devices: 33.2 us -> 26.4 us  [compute(): got = lax.ppermute(sent, 'row', partners(n_row // 2, step))]
    ppermute x4, waiting for transfers between devices: 21 us -> 19.3 us  [compute(): got = lax.ppermute(sent, 'row', partners(n_row // 2, step))]
  transfers between devices with their start and end apart: 11 -> 11, of which waited for: 6 -> 6; matrix products, arithmetic and copies ran while one was open for 0% -> 0% of each run, Pallas kernels for 4% -> 5%
where the time goes in v4:
time: 81.8 us; the launch traced here: 81.4 us
  starting transfers between devices  42.4 us (52%)
  waiting for transfers between devices  29.1 us (36%)
  Pallas kernels  8.25 us (10%)
  between operations  0.89 us (1%)
    ppermute x4, starting transfers between devices, compute(): got = lax.ppermute(sent, 'row', partners(n_row // 2, step))  26.4 us
    ppermute x4, waiting for transfers between devices, compute(): got = lax.ppermute(sent, 'row', partners(n_row // 2, step))  19.3 us
    ppermute x3, starting transfers between devices, exchange(): lax.ppermute(low, axis, forward)  8.73 us
    ppermute x3, waiting for transfers between devices, exchange(): lax.ppermute(high, axis, backward)  7.54 us
    ppermute x3, starting transfers between devices, exchange(): lax.ppermute(high, axis, backward)  3.88 us
    ppermute x1, starting transfers between devices, compute(): got = lax.ppermute(send, 'row', [(i, i ^ 1) for i in range(n_row)])  3.31 us
    pallas_call x1, Pallas kernels, main(): pl.pallas_call(main_kernel, in_specs=[vmem()] * 6 + [hbm()] + [vmem()] *...  2.91 us
    pallas_call x1, Pallas kernels, last(): pl.pallas_call(last_kernel, in_specs=[hbm()] * 3 + [vmem()] * 6, out_spec...  2.57 us
  transfers between devices with their start and end apart: 11, of which 6 were waited for; matrix products, arithmetic and copies ran while one was open for 0% of the time, Pallas kernels for 5%

profile of v4, /device:TPU:4, one launch (start us, length us, event | category | flops | bytes accessed | tf_op | source)
XLA Modules:
  0.0 81.4 jit_solution(17903239504734054049)
XLA Ops:
  0.6 0.0 copy-start
  0.6 0.0 copy-start.2
  0.7 1.2 %edges.1 = (f32[3,1024]{1,0:T(4,128)S(1)}, f32[3,1024]{1,0:T(4,128)S(1)}, f32[1,128]{1,0:T(1,128)S(1)}, f32[1,128]{1,0:T(1,128)S(1)}) custom-call(f32[128,1024]{1,0:T(8,128)} %a_ref.1, f32[128,1024]{1,0:T(8,128)} %a_ref.1, f32[128,1024]{1,0:T(8,128)} %a_ref.1, f32[128,1024]{1,0:T(8,128)} %a_ref.1, f32[128,1024]{1,0:T(8,128)} %kap_hbm.1, ...), custom_call_target="tpu_custom_call" | custom-call | tf_op jit(solution)/shard_map/edges/pallas_call | solution.py:81
  1.9 1.7 %collective-permute-start = (f32[3,1024]{1,0:T(4,128)S(1)}, f32[3,1024]{1,0:T(4,128)S(1)}, u32[]{:S(2)}, u32[]{:S(2)}) collective-permute-start(f32[3,1024]{1,0:T(4,128)S(1)} %get-tuple-element.16.b_ref), channel_id=1, source_target_pairs={{0,16},{16,32},{32,48},{48,64},{64,80},{80,96},{96,112},{112,128},... | collective-permute-start | bytes 36872 | tf_op jit(solution)/shard_map/ppermute | solution.py:380
  3.6 1.3 %collective-permute-start.1 = (f32[3,1024]{1,0:T(4,128)S(1)}, f32[3,1024]{1,0:T(4,128)S(1)}, u32[]{:S(2)}, u32[]{:S(2)}) collective-permute-start(f32[3,1024]{1,0:T(4,128)S(1)} %get-tuple-element.17.t_ref), channel_id=1, source_target_pairs={{16,0},{32,16},{48,32},{64,48},{80,64},{96,80},{112,96},{128,112},... | collective-permute-start | bytes 36872 | tf_op jit(solution)/shard_map/ppermute | solution.py:380
  4.9 3.5 %collective-permute-start.2 = (f32[1,128]{1,0:T(1,128)S(1)}, f32[1,128]{1,0:T(1,128)S(1)}, u32[]{:S(2)}, u32[]{:S(2)}) collective-permute-start(f32[1,128]{1,0:T(1,128)S(1)} %get-tuple-element.18), channel_id=1, source_target_pairs={{0,4},{4,8},{8,12},{1,5},{5,9},{9,13},{2,6},{6,10},{10,14},{3,7},{... | collective-permute-start | bytes 1544 | tf_op jit(solution)/shard_map/ppermute | solution.py:380
  8.4 1.3 %collective-permute-start.3 = (f32[1,128]{1,0:T(1,128)S(1)}, f32[1,128]{1,0:T(1,128)S(1)}, u32[]{:S(2)}, u32[]{:S(2)}) collective-permute-start(f32[1,128]{1,0:T(1,128)S(1)} %get-tuple-element.19), channel_id=1, source_target_pairs={{4,0},{8,4},{12,8},{5,1},{9,5},{13,9},{6,2},{10,6},{14,10},{7,3},{... | collective-permute-start | bytes 1544 | tf_op jit(solution)/shard_map/ppermute | solution.py:380
  9.8 0.7 indices.1
  10.5 0.0 collective-permute-done.2.w_ref
  10.5 3.4 %collective-permute-done.3.e_ref = f32[1,128]{1,0:T(1,128)S(1)} collective-permute-done((f32[1,128]{1,0:T(1,128)S(1)}, f32[1,128]{1,0:T(1,128)S(1)}, u32[]{:S(2)}, u32[]{:S(2)}) %collective-permute-start.3) | collective-permute-done | bytes 544 | tf_op jit(solution)/shard_map/ppermute | solution.py:380
  13.9 0.0 collective-permute-done.n_ref
  13.9 0.0 collective-permute-done.1.s_ref
  13.9 2.9 %main.1 = (f32[128,1024]{1,0:T(8,128)S(1)}, f32[1,256]{1,0:T(1,128)S(1)}, f32[1,256]{1,0:T(1,128)S(1)}, bf16[512,256]{1,0:T(8,128)(2,1)S(1)}, bf16[512,256]{1,0:T(8,128)(2,1)S(1)}, /*index=5*/f32[1024,256]{1,0:T(8,128)S(1)}) custom-call(f32[128,1024]{1,0:T(8,128)S(1)} %copy-done.1, f32[128,1024]{1,0:T(8,128)S(1)} %get-tuple-element.15.coef_ref, ...), custom_call_target="tpu_custom_call" | custom-call | flops 1000000000 | bytes 6291456 | tf_op jit(solution)/shard_map/main/pallas_call | solution.py:271
  16.8 3.3 %collective-permute-start.6 = (f32[1024,256]{1,0:T(8,128)S(1)}, f32[1024,256]{1,0:T(8,128)S(1)}, u32[]{:S(2)}, u32[]{:S(2)}) collective-permute-start(f32[1024,256]{1,0:T(8,128)S(1)} %get-tuple-element.27), channel_id=1, source_target_pairs={{0,16},{16,0},{32,48},{48,32},{64,80},{80,64},{96,112},{112,96},{1... | collective-permute-start | bytes 3145736 | tf_op jit(solution)/shard_map/ppermute | solution.py:412
  20.1 2.3 %collective-permute-done.6.got_ref = f32[1024,256]{1,0:T(8,128)S(1)} collective-permute-done((f32[1024,256]{1,0:T(8,128)S(1)}, f32[1024,256]{1,0:T(8,128)S(1)}, u32[]{:S(2)}, u32[]{:S(2)}) %collective-permute-start.6) | collective-permute-done | bytes 1048608 | tf_op jit(solution)/shard_map/ppermute | solution.py:412
  22.4 0.4 add.44
  22.8 5.3 %collective-permute-start.7 = (f32[512,256]{1,0:T(8,128)S(1)}, f32[512,256]{1,0:T(8,128)S(1)}, u32[]{:S(2)}, u32[]{:S(2)}) collective-permute-start(f32[512,256]{1,0:T(8,128)S(1)} %add.44), channel_id=1, source_target_pairs={{0,32},{16,496},{32,0},{48,80},{64,96},{80,48},{96,64},{112,144},{... | collective-permute-start | bytes 1572872 | tf_op jit(solution)/shard_map/ppermute | solution.py:420
  28.2 0.5 add.43
  28.6 6.7 %collective-permute-done.7 = f32[512,256]{1,0:T(8,128)S(1)} collective-permute-done((f32[512,256]{1,0:T(8,128)S(1)}, f32[512,256]{1,0:T(8,128)S(1)}, u32[]{:S(2)}, u32[]{:S(2)}) %collective-permute-start.7) | collective-permute-done | bytes 524320 | tf_op jit(solution)/shard_map/ppermute | solution.py:420
  35.3 0.1 slice_add_fusion.1
  35.4 11.5 %collective-permute-start.8 = (f32[256,256]{1,0:T(8,128)S(1)}, f32[256,256]{1,0:T(8,128)S(1)}, u32[]{:S(2)}, u32[]{:S(2)}) collective-permute-start(f32[256,256]{1,0:T(8,128)S(1)} %get-tuple-element.29), channel_id=1, source_target_pairs={{0,480},{16,48},{32,64},{48,16},{64,32},{80,112},{96,128},{112,80}... | collective-permute-start | bytes 786440 | tf_op jit(solution)/shard_map/ppermute | solution.py:420
  46.9 4.3 %collective-permute-done.8 = f32[256,256]{1,0:T(8,128)S(1)} collective-permute-done((f32[256,256]{1,0:T(8,128)S(1)}, f32[256,256]{1,0:T(8,128)S(1)}, u32[]{:S(2)}, u32[]{:S(2)}) %collective-permute-start.8) | collective-permute-done | bytes 262176 | tf_op jit(solution)/shard_map/ppermute | solution.py:420
  51.3 1.9 %collective-permute-start.9 = (f32[128,256]{1,0:T(8,128)S(1)}, f32[128,256]{1,0:T(8,128)S(1)}, u32[]{:S(2)}, u32[]{:S(2)}) collective-permute-start(f32[128,256]{1,0:T(8,128)S(1)} %get-tuple-element.31), channel_id=1, source_target_pairs={{0,96},{16,432},{32,448},{48,144},{64,160},{80,496},{96,0},{112,20... | collective-permute-start | bytes 393224 | tf_op jit(solution)/shard_map/ppermute | solution.py:420
  53.2 8.2 %collective-permute-done.9 = f32[128,256]{1,0:T(8,128)S(1)} collective-permute-done((f32[128,256]{1,0:T(8,128)S(1)}, f32[128,256]{1,0:T(8,128)S(1)}, u32[]{:S(2)}, u32[]{:S(2)}) %collective-permute-start.9) | collective-permute-done | bytes 131104 | tf_op jit(solution)/shard_map/ppermute | solution.py:420
  61.4 7.7 %collective-permute-start.10 = (f32[64,256]{1,0:T(8,128)S(1)}, f32[64,256]{1,0:T(8,128)S(1)}, u32[]{:S(2)}, u32[]{:S(2)}) collective-permute-start(f32[64,256]{1,0:T(8,128)S(1)} %slice_add_fusion.4), channel_id=1, source_target_pairs={{0,352},{16,176},{32,192},{48,400},{64,416},{80,240},{96,256},{112... | collective-permute-start | bytes 196616 | tf_op jit(solution)/shard_map/ppermute | solution.py:420
  69.1 3.5 %collective-permute-start.4 = (f32[1,256]{1,0:T(1,128)S(1)}, f32[1,256]{1,0:T(1,128)S(1)}, u32[]{:S(2)}, u32[]{:S(2)}) collective-permute-start(f32[1,256]{1,0:T(1,128)S(1)} %get-tuple-element.23), channel_id=1, source_target_pairs={{0,4},{4,8},{8,12},{1,5},{5,9},{9,13},{2,6},{6,10},{10,14},{3,7},{... | collective-permute-start | bytes 3080 | tf_op jit(solution)/shard_map/ppermute | solution.py:380
  72.7 1.3 %collective-permute-start.5 = (f32[1,256]{1,0:T(1,128)S(1)}, f32[1,256]{1,0:T(1,128)S(1)}, u32[]{:S(2)}, u32[]{:S(2)}) collective-permute-start(f32[1,256]{1,0:T(1,128)S(1)} %get-tuple-element.24), channel_id=1, source_target_pairs={{4,0},{8,4},{12,8},{5,1},{9,5},{13,9},{6,2},{10,6},{14,10},{7,3},{... | collective-permute-start | bytes 3080 | tf_op jit(solution)/shard_map/ppermute | solution.py:380
  74.0 0.0 collective-permute-done.4.w_ref
  74.0 4.2 %collective-permute-done.5.e_ref = f32[1,256]{1,0:T(1,128)S(1)} collective-permute-done((f32[1,256]{1,0:T(1,128)S(1)}, f32[1,256]{1,0:T(1,128)S(1)}, u32[]{:S(2)}, u32[]{:S(2)}) %collective-permute-start.5) | collective-permute-done | bytes 1056 | tf_op jit(solution)/shard_map/ppermute | solution.py:380
  78.1 2.6 %last.1 = f32[128,1024]{1,0:T(8,128)} custom-call(f32[128,1024]{1,0:T(8,128)S(1)} %get-tuple-element.22.a_hbm, f32[128,1024]{1,0:T(8,128)} %kap_hbm.1, f32[128,1024]{1,0:T(8,128)} %elev_hbm.1, f32[3,1024]{1,0:T(4,128)S(1)} %collective-permute-done.n_ref, f32[3,1024]{1,0:T(4,128)S(1)} %collective-permute-done.1.s_ref, ...), custom_call_target="tpu_custom_call" | custom-call | flops 10000000 | bytes 2097152 | tf_op jit(solution)/shard_map/last/pallas_call | solution.py:355
  80.7 0.0 collective-permute-done.10
  80.7 0.6 fusion.1
  (12 shorter events, 0.1 us)
Async XLA Ops:
  0.6 9.1 %copy-start = (f32[128,1024]{1,0:T(8,128)S(1)}, f32[128,1024]{1,0:T(8,128)}, u32[]{:S(2)}) copy-start(f32[128,1024]{1,0:T(8,128)} %kap_hbm.1) | copy-start | bytes 1572868
  0.6 9.1 %copy-start.2 = (f32[128,1024]{1,0:T(8,128)S(1)}, f32[128,1024]{1,0:T(8,128)}, u32[]{:S(2)}) copy-start(f32[128,1024]{1,0:T(8,128)} %ebot_ref.1) | copy-start | bytes 1572868
  0.7 13.2 %copy-start.1 = (f32[128,1024]{1,0:T(8,128)S(1)}, f32[128,1024]{1,0:T(8,128)}, u32[]{:S(2)}) copy-start(f32[128,1024]{1,0:T(8,128)} %a_ref.1) | copy-start | bytes 1572868
  0.7 9.1 %copy-start.3 = (s32[1,2048]{1,0:T(1,128)S(1)}, s32[1,2048]{1,0:T(1,128)}, u32[]{:S(2)}) copy-start(s32[1,2048]{1,0:T(1,128)} %owner_ref.1) | copy-start | bytes 24580
  0.7 9.1 %copy-start.4 = (s32[1,1,512]{2,1,0:T(1,128)S(1)}, s32[1,1,512]{2,1,0:T(1,128)}, u32[]{:S(2)}) copy-start(s32[1,1,512]{2,1,0:T(1,128)} %param.14) | copy-start | bytes 6148
  0.7 9.1 %copy-start.5 = (s32[1,1,512]{2,1,0:T(1,128)S(1)}, s32[1,1,512]{2,1,0:T(1,128)}, u32[]{:S(2)}) copy-start(s32[1,1,512]{2,1,0:T(1,128)} %param.13) | copy-start | bytes 6148
  1.9 12.0 %collective-permute-start = (f32[3,1024]{1,0:T(4,128)S(1)}, f32[3,1024]{1,0:T(4,128)S(1)}, u32[]{:S(2)}, u32[]{:S(2)}) collective-permute-start(f32[3,1024]{1,0:T(4,128)S(1)} %get-tuple-element.16.b_ref), channel_id=1, source_target_pairs={{0,16},{16,32},{32,48},{48,64},{64,80},{80,96},{96,112},{112,128},... | collective-permute-start | bytes 36872 | tf_op jit(solution)/shard_map/ppermute | solution.py:380
  3.6 10.3 %collective-permute-start.1 = (f32[3,1024]{1,0:T(4,128)S(1)}, f32[3,1024]{1,0:T(4,128)S(1)}, u32[]{:S(2)}, u32[]{:S(2)}) collective-permute-start(f32[3,1024]{1,0:T(4,128)S(1)} %get-tuple-element.17.t_ref), channel_id=1, source_target_pairs={{16,0},{32,16},{48,32},{64,48},{80,64},{96,80},{112,96},{128,112},... | collective-permute-start | bytes 36872 | tf_op jit(solution)/shard_map/ppermute | solution.py:380
  4.9 5.6 %collective-permute-start.2 = (f32[1,128]{1,0:T(1,128)S(1)}, f32[1,128]{1,0:T(1,128)S(1)}, u32[]{:S(2)}, u32[]{:S(2)}) collective-permute-start(f32[1,128]{1,0:T(1,128)S(1)} %get-tuple-element.18), channel_id=1, source_target_pairs={{0,4},{4,8},{8,12},{1,5},{5,9},{9,13},{2,6},{6,10},{10,14},{3,7},{... | collective-permute-start | bytes 1544 | tf_op jit(solution)/shard_map/ppermute | solution.py:380
  8.4 5.5 %collective-permute-start.3 = (f32[1,128]{1,0:T(1,128)S(1)}, f32[1,128]{1,0:T(1,128)S(1)}, u32[]{:S(2)}, u32[]{:S(2)}) collective-permute-start(f32[1,128]{1,0:T(1,128)S(1)} %get-tuple-element.19), channel_id=1, source_target_pairs={{4,0},{8,4},{12,8},{5,1},{9,5},{13,9},{6,2},{10,6},{14,10},{7,3},{... | collective-permute-start | bytes 1544 | tf_op jit(solution)/shard_map/ppermute | solution.py:380
  16.8 5.6 %collective-permute-start.6 = (f32[1024,256]{1,0:T(8,128)S(1)}, f32[1024,256]{1,0:T(8,128)S(1)}, u32[]{:S(2)}, u32[]{:S(2)}) collective-permute-start(f32[1024,256]{1,0:T(8,128)S(1)} %get-tuple-element.27), channel_id=1, source_target_pairs={{0,16},{16,0},{32,48},{48,32},{64,80},{80,64},{96,112},{112,96},{1... | collective-permute-start | bytes 3145736 | tf_op jit(solution)/shard_map/ppermute | solution.py:412
  22.8 12.5 %collective-permute-start.7 = (f32[512,256]{1,0:T(8,128)S(1)}, f32[512,256]{1,0:T(8,128)S(1)}, u32[]{:S(2)}, u32[]{:S(2)}) collective-permute-start(f32[512,256]{1,0:T(8,128)S(1)} %add.44), channel_id=1, source_target_pairs={{0,32},{16,496},{32,0},{48,80},{64,96},{80,48},{96,64},{112,144},{... | collective-permute-start | bytes 1572872 | tf_op jit(solution)/shard_map/ppermute | solution.py:420
  35.4 15.8 %collective-permute-start.8 = (f32[256,256]{1,0:T(8,128)S(1)}, f32[256,256]{1,0:T(8,128)S(1)}, u32[]{:S(2)}, u32[]{:S(2)}) collective-permute-start(f32[256,256]{1,0:T(8,128)S(1)} %get-tuple-element.29), channel_id=1, source_target_pairs={{0,480},{16,48},{32,64},{48,16},{64,32},{80,112},{96,128},{112,80}... | collective-permute-start | bytes 786440 | tf_op jit(solution)/shard_map/ppermute | solution.py:420
  51.3 10.2 %collective-permute-start.9 = (f32[128,256]{1,0:T(8,128)S(1)}, f32[128,256]{1,0:T(8,128)S(1)}, u32[]{:S(2)}, u32[]{:S(2)}) collective-permute-start(f32[128,256]{1,0:T(8,128)S(1)} %get-tuple-element.31), channel_id=1, source_target_pairs={{0,96},{16,432},{32,448},{48,144},{64,160},{80,496},{96,0},{112,20... | collective-permute-start | bytes 393224 | tf_op jit(solution)/shard_map/ppermute | solution.py:420
  61.4 19.3 %collective-permute-start.10 = (f32[64,256]{1,0:T(8,128)S(1)}, f32[64,256]{1,0:T(8,128)S(1)}, u32[]{:S(2)}, u32[]{:S(2)}) collective-permute-start(f32[64,256]{1,0:T(8,128)S(1)} %slice_add_fusion.4), channel_id=1, source_target_pairs={{0,352},{16,176},{32,192},{48,400},{64,416},{80,240},{96,256},{112... | collective-permute-start | bytes 196616 | tf_op jit(solution)/shard_map/ppermute | solution.py:420
  69.1 4.8 %collective-permute-start.4 = (f32[1,256]{1,0:T(1,128)S(1)}, f32[1,256]{1,0:T(1,128)S(1)}, u32[]{:S(2)}, u32[]{:S(2)}) collective-permute-start(f32[1,256]{1,0:T(1,128)S(1)} %get-tuple-element.23), channel_id=1, source_target_pairs={{0,4},{4,8},{8,12},{1,5},{5,9},{9,13},{2,6},{6,10},{10,14},{3,7},{... | collective-permute-start | bytes 3080 | tf_op jit(solution)/shard_map/ppermute | solution.py:380
  72.7 5.5 %collective-permute-start.5 = (f32[1,256]{1,0:T(1,128)S(1)}, f32[1,256]{1,0:T(1,128)S(1)}, u32[]{:S(2)}, u32[]{:S(2)}) collective-permute-start(f32[1,256]{1,0:T(1,128)S(1)} %get-tuple-element.24), channel_id=1, source_target_pairs={{4,0},{8,4},{12,8},{5,1},{9,5},{13,9},{6,2},{10,6},{14,10},{7,3},{... | collective-permute-start | bytes 3080 | tf_op jit(solution)/shard_map/ppermute | solution.py:380

commit v5 on v4

--- a/solution.py
+++ b/solution.py
@@ -58,30 +58,34 @@
 
 
 def edges_kernel(
-    top_ref, bot_ref, left_ref, right_ref, ktop_ref, kbot_ref, etop_ref, ebot_ref,
+    n_row, n_col, place_ref, col_ref, top_ref, bot_ref, left_ref, right_ref, ktop_ref, kbot_ref, etop_ref, ebot_ref,
     t_ref, b_ref, l_ref, r_ref,
 ):
     top, bot = top_ref[...], bot_ref[...]
     partial, coef = edge_row(top, pltpu.roll(top, 7, 0), ktop_ref[...], etop_ref[...])
-    t_ref[0:1, :] = top[0:1, :]
-    t_ref[1:2, :] = partial[0:1, :]
-    t_ref[2:3, :] = coef[0:1, :]
+    inside = place_ref[0] > 0
+    t_ref[0:1, :] = jnp.where(inside, top[0:1, :], 0.0)
+    t_ref[1:2, :] = jnp.where(inside, partial[0:1, :], 0.0)
+    t_ref[2:3, :] = jnp.where(inside, coef[0:1, :], 0.0)
     partial, coef = edge_row(bot, pltpu.roll(bot, 1, 0), kbot_ref[...], ebot_ref[...])
-    b_ref[0:1, :] = bot[7:8, :]
-    b_ref[1:2, :] = partial[7:8, :]
-    b_ref[2:3, :] = coef[7:8, :]
-    l_ref[...] = left_ref[...].T[0:1, :]
-    r_ref[...] = right_ref[...].T[127:128, :]
-
-
-def edges(a, kappa, elev):
+    inside = place_ref[0] < n_row - 1
+    b_ref[0:1, :] = jnp.where(inside, bot[7:8, :], 0.0)
+    b_ref[1:2, :] = jnp.where(inside, partial[7:8, :], 0.0)
+    b_ref[2:3, :] = jnp.where(inside, coef[7:8, :], 0.0)
+    l_ref[...] = jnp.where(col_ref[0] > 0, left_ref[...].T[0:1, :], 0.0)
+    r_ref[...] = jnp.where(col_ref[0] < n_col - 1, right_ref[...].T[127:128, :], 0.0)
+
+
+def edges(n_row, n_col, place, col, a, kappa, elev):
     rows, cols = a.shape
     first = pl.BlockSpec((8, cols), lambda i: (0, 0))
     final = pl.BlockSpec((8, cols), lambda i: (rows // 8 - 1, 0))
     return pl.pallas_call(
-        edges_kernel,
+        functools.partial(edges_kernel, n_row, n_col),
         grid=(1,),
         in_specs=[
+            pl.BlockSpec(memory_space=pltpu.SMEM),
+            pl.BlockSpec(memory_space=pltpu.SMEM),
             first,
             final,
             pl.BlockSpec((rows, 128), lambda i: (0, 0)),
@@ -100,7 +104,7 @@
         out_shape=[whole((3, cols)), whole((3, cols)), whole((1, rows)), whole((1, rows))],
         compiler_params=params(4 << 20),
         name="edges",
-    )(a, a, a, a, kappa, kappa, elev, elev)
+    )(place, col, a, a, a, a, kappa, kappa, elev, elev)
 
 
 def index_kernel(
@@ -198,7 +202,7 @@
 
 
 def main_kernel(
-    a_ref, coef_ref, n_ref, s_ref, w_ref, e_ref, basis_ref, dest_ref, sel_ref,
+    n_col, col_ref, a_ref, coef_ref, n_ref, s_ref, w_ref, e_ref, basis_ref, dest_ref, sel_ref,
     mid_hbm, l_ref, r_ref, hi_ref, lo_ref, send_ref,
     wt, et, g_ref, y_ref, c_ref, table, mid_ref, sems,
 ):
@@ -255,22 +259,25 @@
     hi_ref[...] = hi
     lo_ref[...] = lo
     gather_rows(send_ref, dest_ref[...], hi, lo, send_ref.shape[0])
-    l_ref[:, 0:128] = mid_ref[:, 0:128].T[0:1, :]
-    r_ref[:, 0:128] = mid_ref[:, cols - 128 : cols].T[127:128, :]
     lane = lax.broadcasted_iota(I32, (1, 128), 1)
+    column_of = {0: mid_ref[:, 0:128].T[0:1, :]}
+    column_of[cols - 1] = mid_ref[:, cols - 128 : cols].T[127:128, :]
     for out, k in ((l_ref, 0), (r_ref, cols - 1)):
+        inside = (col_ref[0] > 0) if k == 0 else (col_ref[0] < n_col - 1)
         corner = jnp.where(lane == 1, south[:, k : k + 1], 0.0)
-        out[:, 128:256] = jnp.where(lane == 0, north[:, k : k + 1], corner)
+        corner = jnp.where(lane == 0, north[:, k : k + 1], corner)
+        out[:, 0:128] = jnp.where(inside, column_of[k], 0.0)
+        out[:, 128:256] = jnp.where(inside, corner, 0.0)
     stored.wait()
 
 
-def main(a, coef, halo, basis, dest, sel, total):
+def main(n_col, col, a, coef, halo, basis, dest, sel, total):
     rows, cols = a.shape
     entries = dest.shape[1]
     ncoef = basis.shape[-1]
     return pl.pallas_call(
-        main_kernel,
-        in_specs=[vmem()] * 6 + [hbm()] + [vmem()] * 2,
+        functools.partial(main_kernel, n_col),
+        in_specs=[pl.BlockSpec(memory_space=pltpu.SMEM)] + [vmem()] * 6 + [hbm()] + [vmem()] * 2,
         out_specs=[hbm()] + [vmem()] * 5,
         out_shape=[
             whole((rows, cols)),
@@ -295,7 +302,7 @@
             flops=10**9, bytes_accessed=6 << 20, transcendentals=0
         ),
         name="main",
-    )(a, coef, *halo, basis, dest, sel)
+    )(col, a, coef, *halo, basis, dest, sel)
 
 
 def add_kernel(first, dest_ref, hi_ref, lo_ref, got_ref, out_ref):
@@ -375,7 +382,7 @@
 
 def exchange(axis, low, high):
     count = lax.axis_size(axis)
-    forward = [(i, i + 1) for i in range(count - 1)]
+    forward = [(i, (i + 1) % count) for i in range(count)]
     backward = [(target, source) for source, target in forward]
     return [lax.ppermute(low, axis, forward), lax.ppermute(high, axis, backward)]
 
@@ -399,15 +406,21 @@
 ):
     n_row = lax.axis_size("row")
     total = owner_row.shape[1]
+    n_col = lax.axis_size("col")
     place = lax.axis_index("row").astype(I32)
-    top, bottom, left, right = edges(in_hbm(adj_final), in_hbm(kappa), in_hbm(elev_late))
+    col = lax.axis_index("col").astype(I32).reshape(1)
+    top, bottom, left, right = edges(
+        n_row, n_col, place.reshape(1), col, in_hbm(adj_final), in_hbm(kappa),
+        in_hbm(elev_late),
+    )
+    halo_col = exchange("col", right, left)
     halo_row = exchange("row", bottom, top)
-    halo = halo_row + exchange("col", right, left)
+    halo = halo_row + halo_col
     dest, sel, coef = indices(
         place.reshape(1), intersection_patch[0], owner_row, basis_index[0], kappa, elev_late
     )
     mid, left, right, hi, lo, send = main(
-        adj_final, coef, halo, in_hbm(basis[0, 0]), dest, sel, total
+        n_col, col, adj_final, coef, halo, in_hbm(basis[0, 0]), dest, sel, total
     )
     got = lax.ppermute(send, "row", [(i, i ^ 1) for i in range(n_row)])
     half = got.shape[0] // 2

time: 81.8 us -> 77.9 us (0.952)
  the two profiles are of different devices: /device:TPU:4 before, /device:TPU:2 now
where the time goes in v5:
time: 77.9 us; the launch traced here: 77.5 us
  starting transfers between devices  39.5 us (51%)
  waiting for transfers between devices  28.1 us (36%)
  Pallas kernels  8.27 us (11%)
  between operations  0.88 us (1%)
    ppermute x4, waiting for transfers between devices, compute(): got = lax.ppermute(sent, 'row', partners(n_row // 2, step))  22.5 us
    ppermute x3, starting transfers between devices, exchange(): lax.ppermute(high, axis, backward)  16.1 us
    ppermute x4, starting transfers between devices, compute(): got = lax.ppermute(sent, 'row', partners(n_row // 2, step))  14.5 us
    ppermute x3, starting transfers between devices, exchange(): lax.ppermute(low, axis, forward)  6.97 us
    ppermute x3, waiting for transfers between devices, exchange(): lax.ppermute(high, axis, backward)  2.97 us
    pallas_call x1, Pallas kernels, main(): pl.pallas_call(functools.partial(main_kernel, n_col), in_specs=[pl.BlockS...  2.92 us
    ppermute x1, waiting for transfers between devices, compute(): got = lax.ppermute(send, 'row', [(i, i ^ 1) for i in range(n_row)])  2.63 us
    pallas_call x1, Pallas kernels, last(): pl.pallas_call(last_kernel, in_specs=[hbm()] * 3 + [vmem()] * 6, out_spec...  2.57 us
  transfers between devices with their start and end apart: 11, of which 6 were waited for; matrix products, arithmetic and copies ran while one was open for 0% of the time, Pallas kernels for 5%

profile of v5, /device:TPU:2, one launch (start us, length us, event | category | flops | bytes accessed | tf_op | source)
XLA Modules:
  0.0 77.5 jit_solution(8450980018259717915)
XLA Ops:
  0.6 0.0 copy-start.1
  0.6 0.0 copy-start.2
  0.7 1.2 %edges.1 = (f32[3,1024]{1,0:T(4,128)S(1)}, f32[3,1024]{1,0:T(4,128)S(1)}, f32[1,128]{1,0:T(1,128)S(1)}, f32[1,128]{1,0:T(1,128)S(1)}) custom-call(s32[1]{0:T(128)} %bitcast.1.place_ref, s32[1]{0:T(128)} %bitcast.col_ref, f32[128,1024]{1,0:T(8,128)} %a_ref.1, f32[128,1024]{1,0:T(8,128)} %a_ref.1, f32[128,1024]{1,0:T(8,128)} %a_ref.1, f32[128,1024]{1,0:T(8,128)} %a_ref.1, ...), custom_call_target="tpu_custom_call" | custom-call | tf_op jit(solution)/shard_map/edges/pallas_call | solution.py:83
  1.9 0.0 collective-permute-start
  1.9 8.9 %collective-permute-start.1 = (f32[3,1024]{1,0:T(4,128)S(1)}, f32[3,1024]{1,0:T(4,128)S(1)}, u32[]{:S(2)}, u32[]{:S(2)}) collective-permute-start(f32[3,1024]{1,0:T(4,128)S(1)} %get-tuple-element.17.t_ref), channel_id=1, source_target_pairs={{16,0},{32,16},{48,32},{64,48},{80,64},{96,80},{112,96},{128,112},... | collective-permute-start | bytes 36872 | tf_op jit(solution)/shard_map/ppermute | solution.py:387
  10.8 3.5 %collective-permute-start.2 = (f32[1,128]{1,0:T(1,128)S(1)}, f32[1,128]{1,0:T(1,128)S(1)}, u32[]{:S(2)}, u32[]{:S(2)}) collective-permute-start(f32[1,128]{1,0:T(1,128)S(1)} %get-tuple-element.18), channel_id=1, source_target_pairs={{0,4},{4,8},{8,12},{12,0},{1,5},{5,9},{9,13},{13,1},{2,6},{6,10},{... | collective-permute-start | bytes 1544 | tf_op jit(solution)/shard_map/ppermute | solution.py:387
  14.3 3.6 %collective-permute-start.3 = (f32[1,128]{1,0:T(1,128)S(1)}, f32[1,128]{1,0:T(1,128)S(1)}, u32[]{:S(2)}, u32[]{:S(2)}) collective-permute-start(f32[1,128]{1,0:T(1,128)S(1)} %get-tuple-element.19), channel_id=1, source_target_pairs={{4,0},{8,4},{12,8},{0,12},{5,1},{9,5},{13,9},{1,13},{6,2},{10,6},{... | collective-permute-start | bytes 1544 | tf_op jit(solution)/shard_map/ppermute | solution.py:387
  18.0 0.7 indices.1
  18.7 0.0 collective-permute-done.2.w_ref
  18.7 1.1 %collective-permute-done.3.e_ref = f32[1,128]{1,0:T(1,128)S(1)} collective-permute-done((f32[1,128]{1,0:T(1,128)S(1)}, f32[1,128]{1,0:T(1,128)S(1)}, u32[]{:S(2)}, u32[]{:S(2)}) %collective-permute-start.3) | collective-permute-done | bytes 544 | tf_op jit(solution)/shard_map/ppermute | solution.py:387
  19.8 0.0 collective-permute-done.n_ref
  19.8 0.0 collective-permute-done.1.s_ref
  19.8 2.9 %main.1 = (f32[128,1024]{1,0:T(8,128)S(1)}, f32[1,256]{1,0:T(1,128)S(1)}, f32[1,256]{1,0:T(1,128)S(1)}, bf16[512,256]{1,0:T(8,128)(2,1)S(1)}, bf16[512,256]{1,0:T(8,128)(2,1)S(1)}, /*index=5*/f32[1024,256]{1,0:T(8,128)S(1)}) custom-call(s32[1]{0:T(128)} %bitcast.col_ref, f32[128,1024]{1,0:T(8,128)S(1)} %copy-done, ...), custom_call_target="tpu_custom_call" | custom-call | flops 1000000000 | bytes 6291456 | tf_op jit(solution)/shard_map/main/pallas_call | solution.py:278
  22.7 1.9 %collective-permute-start.6 = (f32[1024,256]{1,0:T(8,128)S(1)}, f32[1024,256]{1,0:T(8,128)S(1)}, u32[]{:S(2)}, u32[]{:S(2)}) collective-permute-start(f32[1024,256]{1,0:T(8,128)S(1)} %get-tuple-element.27), channel_id=1, source_target_pairs={{0,16},{16,0},{32,48},{48,32},{64,80},{80,64},{96,112},{112,96},{1... | collective-permute-start | bytes 3145736 | tf_op jit(solution)/shard_map/ppermute | solution.py:425
  24.7 2.6 %collective-permute-done.6.got_ref = f32[1024,256]{1,0:T(8,128)S(1)} collective-permute-done((f32[1024,256]{1,0:T(8,128)S(1)}, f32[1024,256]{1,0:T(8,128)S(1)}, u32[]{:S(2)}, u32[]{:S(2)}) %collective-permute-start.6) | collective-permute-done | bytes 1048608 | tf_op jit(solution)/shard_map/ppermute | solution.py:425
  27.3 0.4 add.44
  27.7 1.9 %collective-permute-start.7 = (f32[512,256]{1,0:T(8,128)S(1)}, f32[512,256]{1,0:T(8,128)S(1)}, u32[]{:S(2)}, u32[]{:S(2)}) collective-permute-start(f32[512,256]{1,0:T(8,128)S(1)} %add.44), channel_id=1, source_target_pairs={{0,32},{16,496},{32,0},{48,80},{64,96},{80,48},{96,64},{112,144},{... | collective-permute-start | bytes 1572872 | tf_op jit(solution)/shard_map/ppermute | solution.py:433
  29.7 0.4 add.43
  30.1 8.7 %collective-permute-done.7 = f32[512,256]{1,0:T(8,128)S(1)} collective-permute-done((f32[512,256]{1,0:T(8,128)S(1)}, f32[512,256]{1,0:T(8,128)S(1)}, u32[]{:S(2)}, u32[]{:S(2)}) %collective-permute-start.7) | collective-permute-done | bytes 524320 | tf_op jit(solution)/shard_map/ppermute | solution.py:433
  38.8 0.1 slice_add_fusion.1
  38.9 4.2 %collective-permute-start.8 = (f32[256,256]{1,0:T(8,128)S(1)}, f32[256,256]{1,0:T(8,128)S(1)}, u32[]{:S(2)}, u32[]{:S(2)}) collective-permute-start(f32[256,256]{1,0:T(8,128)S(1)} %get-tuple-element.29), channel_id=1, source_target_pairs={{0,480},{16,48},{32,64},{48,16},{64,32},{80,112},{96,128},{112,80}... | collective-permute-start | bytes 786440 | tf_op jit(solution)/shard_map/ppermute | solution.py:433
  43.1 5.3 %collective-permute-done.8 = f32[256,256]{1,0:T(8,128)S(1)} collective-permute-done((f32[256,256]{1,0:T(8,128)S(1)}, f32[256,256]{1,0:T(8,128)S(1)}, u32[]{:S(2)}, u32[]{:S(2)}) %collective-permute-start.8) | collective-permute-done | bytes 262176 | tf_op jit(solution)/shard_map/ppermute | solution.py:433
  48.4 1.9 %collective-permute-start.9 = (f32[128,256]{1,0:T(8,128)S(1)}, f32[128,256]{1,0:T(8,128)S(1)}, u32[]{:S(2)}, u32[]{:S(2)}) collective-permute-start(f32[128,256]{1,0:T(8,128)S(1)} %get-tuple-element.31), channel_id=1, source_target_pairs={{0,96},{16,432},{32,448},{48,144},{64,160},{80,496},{96,0},{112,20... | collective-permute-start | bytes 393224 | tf_op jit(solution)/shard_map/ppermute | solution.py:433
  50.3 8.5 %collective-permute-done.9 = f32[128,256]{1,0:T(8,128)S(1)} collective-permute-done((f32[128,256]{1,0:T(8,128)S(1)}, f32[128,256]{1,0:T(8,128)S(1)}, u32[]{:S(2)}, u32[]{:S(2)}) %collective-permute-start.9) | collective-permute-done | bytes 131104 | tf_op jit(solution)/shard_map/ppermute | solution.py:433
  58.9 6.5 %collective-permute-start.10 = (f32[64,256]{1,0:T(8,128)S(1)}, f32[64,256]{1,0:T(8,128)S(1)}, u32[]{:S(2)}, u32[]{:S(2)}) collective-permute-start(f32[64,256]{1,0:T(8,128)S(1)} %slice_add_fusion.4), channel_id=1, source_target_pairs={{0,352},{16,176},{32,192},{48,400},{64,416},{80,240},{96,256},{112... | collective-permute-start | bytes 196616 | tf_op jit(solution)/shard_map/ppermute | solution.py:433
  65.3 3.5 %collective-permute-start.4 = (f32[1,256]{1,0:T(1,128)S(1)}, f32[1,256]{1,0:T(1,128)S(1)}, u32[]{:S(2)}, u32[]{:S(2)}) collective-permute-start(f32[1,256]{1,0:T(1,128)S(1)} %get-tuple-element.23), channel_id=1, source_target_pairs={{0,4},{4,8},{8,12},{12,0},{1,5},{5,9},{9,13},{13,1},{2,6},{6,10},{... | collective-permute-start | bytes 3080 | tf_op jit(solution)/shard_map/ppermute | solution.py:387
  68.8 3.6 %collective-permute-start.5 = (f32[1,256]{1,0:T(1,128)S(1)}, f32[1,256]{1,0:T(1,128)S(1)}, u32[]{:S(2)}, u32[]{:S(2)}) collective-permute-start(f32[1,256]{1,0:T(1,128)S(1)} %get-tuple-element.24), channel_id=1, source_target_pairs={{4,0},{8,4},{12,8},{0,12},{5,1},{9,5},{13,9},{1,13},{6,2},{10,6},{... | collective-permute-start | bytes 3080 | tf_op jit(solution)/shard_map/ppermute | solution.py:387
  72.4 0.0 collective-permute-done.4.w_ref
  72.4 1.9 %collective-permute-done.5.e_ref = f32[1,256]{1,0:T(1,128)S(1)} collective-permute-done((f32[1,256]{1,0:T(1,128)S(1)}, f32[1,256]{1,0:T(1,128)S(1)}, u32[]{:S(2)}, u32[]{:S(2)}) %collective-permute-start.5) | collective-permute-done | bytes 1056 | tf_op jit(solution)/shard_map/ppermute | solution.py:387
  74.3 2.6 %last.1 = f32[128,1024]{1,0:T(8,128)} custom-call(f32[128,1024]{1,0:T(8,128)S(1)} %get-tuple-element.22.a_hbm, f32[128,1024]{1,0:T(8,128)} %kap_hbm.1, f32[128,1024]{1,0:T(8,128)} %elev_hbm.1, f32[3,1024]{1,0:T(4,128)S(1)} %collective-permute-done.n_ref, f32[3,1024]{1,0:T(4,128)S(1)} %collective-permute-done.1.s_ref, ...), custom_call_target="tpu_custom_call" | custom-call | flops 10000000 | bytes 2097152 | tf_op jit(solution)/shard_map/last/pallas_call | solution.py:362
  76.9 0.0 collective-permute-done.10
  76.9 0.6 fusion.1
  (12 shorter events, 0.1 us)
Async XLA Ops:
  0.6 17.3 %copy-start.1 = (f32[128,1024]{1,0:T(8,128)S(1)}, f32[128,1024]{1,0:T(8,128)}, u32[]{:S(2)}) copy-start(f32[128,1024]{1,0:T(8,128)} %kap_hbm.1) | copy-start | bytes 1572868
  0.6 17.3 %copy-start.2 = (f32[128,1024]{1,0:T(8,128)S(1)}, f32[128,1024]{1,0:T(8,128)}, u32[]{:S(2)}) copy-start(f32[128,1024]{1,0:T(8,128)} %ebot_ref.1) | copy-start | bytes 1572868
  0.7 17.3 %copy-start.3 = (s32[1,2048]{1,0:T(1,128)S(1)}, s32[1,2048]{1,0:T(1,128)}, u32[]{:S(2)}) copy-start(s32[1,2048]{1,0:T(1,128)} %owner_ref.1) | copy-start | bytes 24580
  0.7 17.3 %copy-start.4 = (s32[1,1,512]{2,1,0:T(1,128)S(1)}, s32[1,1,512]{2,1,0:T(1,128)}, u32[]{:S(2)}) copy-start(s32[1,1,512]{2,1,0:T(1,128)} %param.14) | copy-start | bytes 6148
  0.7 17.3 %copy-start.5 = (s32[1,1,512]{2,1,0:T(1,128)S(1)}, s32[1,1,512]{2,1,0:T(1,128)}, u32[]{:S(2)}) copy-start(s32[1,1,512]{2,1,0:T(1,128)} %param.13) | copy-start | bytes 6148
  0.7 19.1 %copy-start = (f32[128,1024]{1,0:T(8,128)S(1)}, f32[128,1024]{1,0:T(8,128)}, u32[]{:S(2)}) copy-start(f32[128,1024]{1,0:T(8,128)} %a_ref.1) | copy-start | bytes 1572868
  1.9 17.9 %collective-permute-start = (f32[3,1024]{1,0:T(4,128)S(1)}, f32[3,1024]{1,0:T(4,128)S(1)}, u32[]{:S(2)}, u32[]{:S(2)}) collective-permute-start(f32[3,1024]{1,0:T(4,128)S(1)} %get-tuple-element.16.b_ref), channel_id=1, source_target_pairs={{0,16},{16,32},{32,48},{48,64},{64,80},{80,96},{96,112},{112,128},... | collective-permute-start | bytes 36872 | tf_op jit(solution)/shard_map/ppermute | solution.py:387
  1.9 17.9 %collective-permute-start.1 = (f32[3,1024]{1,0:T(4,128)S(1)}, f32[3,1024]{1,0:T(4,128)S(1)}, u32[]{:S(2)}, u32[]{:S(2)}) collective-permute-start(f32[3,1024]{1,0:T(4,128)S(1)} %get-tuple-element.17.t_ref), channel_id=1, source_target_pairs={{16,0},{32,16},{48,32},{64,48},{80,64},{96,80},{112,96},{128,112},... | collective-permute-start | bytes 36872 | tf_op jit(solution)/shard_map/ppermute | solution.py:387
  10.8 7.8 %collective-permute-start.2 = (f32[1,128]{1,0:T(1,128)S(1)}, f32[1,128]{1,0:T(1,128)S(1)}, u32[]{:S(2)}, u32[]{:S(2)}) collective-permute-start(f32[1,128]{1,0:T(1,128)S(1)} %get-tuple-element.18), channel_id=1, source_target_pairs={{0,4},{4,8},{8,12},{12,0},{1,5},{5,9},{9,13},{13,1},{2,6},{6,10},{... | collective-permute-start | bytes 1544 | tf_op jit(solution)/shard_map/ppermute | solution.py:387
  14.3 5.5 %collective-permute-start.3 = (f32[1,128]{1,0:T(1,128)S(1)}, f32[1,128]{1,0:T(1,128)S(1)}, u32[]{:S(2)}, u32[]{:S(2)}) collective-permute-start(f32[1,128]{1,0:T(1,128)S(1)} %get-tuple-element.19), channel_id=1, source_target_pairs={{4,0},{8,4},{12,8},{0,12},{5,1},{9,5},{13,9},{1,13},{6,2},{10,6},{... | collective-permute-start | bytes 1544 | tf_op jit(solution)/shard_map/ppermute | solution.py:387
  22.7 4.6 %collective-permute-start.6 = (f32[1024,256]{1,0:T(8,128)S(1)}, f32[1024,256]{1,0:T(8,128)S(1)}, u32[]{:S(2)}, u32[]{:S(2)}) collective-permute-start(f32[1024,256]{1,0:T(8,128)S(1)} %get-tuple-element.27), channel_id=1, source_target_pairs={{0,16},{16,0},{32,48},{48,32},{64,80},{80,64},{96,112},{112,96},{1... | collective-permute-start | bytes 3145736 | tf_op jit(solution)/shard_map/ppermute | solution.py:425
  27.7 11.1 %collective-permute-start.7 = (f32[512,256]{1,0:T(8,128)S(1)}, f32[512,256]{1,0:T(8,128)S(1)}, u32[]{:S(2)}, u32[]{:S(2)}) collective-permute-start(f32[512,256]{1,0:T(8,128)S(1)} %add.44), channel_id=1, source_target_pairs={{0,32},{16,496},{32,0},{48,80},{64,96},{80,48},{96,64},{112,144},{... | collective-permute-start | bytes 1572872 | tf_op jit(solution)/shard_map/ppermute | solution.py:433
  38.9 9.5 %collective-permute-start.8 = (f32[256,256]{1,0:T(8,128)S(1)}, f32[256,256]{1,0:T(8,128)S(1)}, u32[]{:S(2)}, u32[]{:S(2)}) collective-permute-start(f32[256,256]{1,0:T(8,128)S(1)} %get-tuple-element.29), channel_id=1, source_target_pairs={{0,480},{16,48},{32,64},{48,16},{64,32},{80,112},{96,128},{112,80}... | collective-permute-start | bytes 786440 | tf_op jit(solution)/shard_map/ppermute | solution.py:433
  48.4 10.5 %collective-permute-start.9 = (f32[128,256]{1,0:T(8,128)S(1)}, f32[128,256]{1,0:T(8,128)S(1)}, u32[]{:S(2)}, u32[]{:S(2)}) collective-permute-start(f32[128,256]{1,0:T(8,128)S(1)} %get-tuple-element.31), channel_id=1, source_target_pairs={{0,96},{16,432},{32,448},{48,144},{64,160},{80,496},{96,0},{112,20... | collective-permute-start | bytes 393224 | tf_op jit(solution)/shard_map/ppermute | solution.py:433
  58.9 18.0 %collective-permute-start.10 = (f32[64,256]{1,0:T(8,128)S(1)}, f32[64,256]{1,0:T(8,128)S(1)}, u32[]{:S(2)}, u32[]{:S(2)}) collective-permute-start(f32[64,256]{1,0:T(8,128)S(1)} %slice_add_fusion.4), channel_id=1, source_target_pairs={{0,352},{16,176},{32,192},{48,400},{64,416},{80,240},{96,256},{112... | collective-permute-start | bytes 196616 | tf_op jit(solution)/shard_map/ppermute | solution.py:433
  65.3 7.1 %collective-permute-start.4 = (f32[1,256]{1,0:T(1,128)S(1)}, f32[1,256]{1,0:T(1,128)S(1)}, u32[]{:S(2)}, u32[]{:S(2)}) collective-permute-start(f32[1,256]{1,0:T(1,128)S(1)} %get-tuple-element.23), channel_id=1, source_target_pairs={{0,4},{4,8},{8,12},{12,0},{1,5},{5,9},{9,13},{13,1},{2,6},{6,10},{... | collective-permute-start | bytes 3080 | tf_op jit(solution)/shard_map/ppermute | solution.py:387
  68.8 5.5 %collective-permute-start.5 = (f32[1,256]{1,0:T(1,128)S(1)}, f32[1,256]{1,0:T(1,128)S(1)}, u32[]{:S(2)}, u32[]{:S(2)}) collective-permute-start(f32[1,256]{1,0:T(1,128)S(1)} %get-tuple-element.24), channel_id=1, source_target_pairs={{4,0},{8,4},{12,8},{0,12},{5,1},{9,5},{13,9},{1,13},{6,2},{10,6},{... | collective-permute-start | bytes 3080 | tf_op jit(solution)/shard_map/ppermute | solution.py:387
